TPU v7x, 128 devices: a whole 4x4x4 slice. The times are simulated.
128 devices in a mesh: lon: 64 (over z, x, y), lev: 2 (over core).
Axes of the slice: x: 4, y: 4, z: 4, core: 2. Of those that a mesh axis runs over, the one named last changes fastest.
Arguments:
- ensemble: float32 [80, 16, 65536], P(None, 'lev', 'lon'), may hold values from -6 to 6
- obs_cell: int32 [12, 128], P(None, 'lon'), may hold values from 0 to 65535, as said below
- obs_value: float32 [12, 128], P(None, 'lon'), may hold values from -5 to 5
- obs_noise: float32 [12, 128], P(None, 'lon'), may hold values from 0.2 to 2
- obs_weight: float32 [12, 16, 128], P(None, 'lev'), may hold values from 0.05 to 0.5
- tile_lists: int32 [12, 1536], P(None, 'lon'), may hold values from 0 to 128, as said below
- batch_order: int32 [12], replicated, may hold values from 0 to 11, each once
Outputs:
- analysis: float32 [80, 16, 65536], P(None, 'lev', 'lon')
Inputs may be any that keep to these rules, and one draw needn't show every extreme that they name: `obs_cell`: each tile holds at most 8 observations of one block, and some tile exactly 8. `tile_lists`: for block b and tile t the tile's 24 slots hold first, ascending and once each, the observations of block b whose tile is t or a neighbour of t around the globe, then the value 128 in every remaining slot; in every block some tile has all 24 slots used. `batch_order`: each block once.
All inputs are finite; a program needn't handle non-finite values.
Results may differ from a plain program's by a relative error of at most 0.0003.
Values sent between devices are 32-bit elements; how exact they have to be, the bound alone decides.
No kernel may reach another device: no remote copies, remote signals or barrier semaphores. Data moves between devices by JAX's collectives and lax.ppermute only.
A program may use at most 128 MiB of HBM per device.

v0:
```python
import jax
import jax.numpy as jnp
from jax import lax
from jax.sharding import Mesh
from jax.sharding import PartitionSpec as P

MEM = 80
OBS = 128
ROUTE_CAP = 24
LON_DEV = 16
CELL_DEV = 1024
BATCHES = 12
LON = ("lon_0", "lon_1", "lon_2")
LON_LEV = ("lon_0", "lon_1", "lon_2", "lev")


highest = lax.Precision.HIGHEST


def joined_along(parts, dim):
    lengths = list(parts.shape[1:])
    lengths[dim] *= parts.shape[0]
    return jnp.moveaxis(parts, 0, dim).reshape(lengths)


def sent_to_all(array, axis):
    copies = jnp.broadcast_to(array, (lax.axis_size(axis), *array.shape))
    return lax.all_to_all(copies, axis, split_axis=0, concat_axis=0, tiled=True)


def collect(array, axis, dim):
    return joined_along(sent_to_all(array, axis), dim)


def rows_first(arrays, axis, dims):
    turned = [jnp.moveaxis(a, dim, 0) for a, dim in zip(arrays, dims)]
    widths = [t[0].size for t in turned]
    both = jnp.concatenate([t.reshape(-1, w) for t, w in zip(turned, widths)], axis=1)
    result = lax.all_gather(both, axis, axis=0, tiled=True)
    parts = jnp.split(result, [sum(widths[:k]) for k in range(1, len(widths))], axis=1)
    return tuple(
        (
            jnp.moveaxis(b.reshape(-1, *t.shape[1:]), 0, dim)
            for b, t, dim in zip(parts, turned, dims)
        )
    )


def filled_up(lines, count):
    spare = -len(lines) % count
    return jnp.pad(lines, [(0, spare)] + [(0, 0)] * (lines.ndim - 1))


def own_block(parts, axes, order):
    inside = parts.shape[1:]
    parts = parts.reshape(*(lax.axis_size(a) for a in axes), *inside)
    parts = jnp.moveaxis(parts, order, range(len(axes))).reshape(-1, *inside)
    for k in order:
        parts = lax.psum_scatter(parts, axes[k], scatter_dimension=0, tiled=True)
    return parts[0]


def gather_in_order(array, axes, order):
    parts = array[None]
    for k in order:
        parts = lax.all_gather(parts, axes[k], axis=0, tiled=True)
    block = [lax.axis_size(axes[k]) for k in reversed(order)]
    parts = parts.reshape(*block, *array.shape)
    turned = sorted(range(len(order)), key=lambda place: order[len(order) - 1 - place])
    return parts.transpose(*turned, *range(len(order), parts.ndim)).reshape(-1, *array.shape)


def sum_in_two_steps(array, axes, order):
    count, lines = (lax.axis_size(axes), array.reshape(-1, *array.shape[1:][-1:]))
    parts = filled_up(lines, count).reshape(count, -1, *lines.shape[1:])
    own = own_block(parts, axes, order)
    whole = gather_in_order(own, axes, order[::-1]).reshape(-1, *lines.shape[1:])
    return whole[: len(lines)].reshape(array.shape)


def locate(cell_ids):
    within = cell_ids % CELL_DEV
    return (within // LON_DEV, cell_ids // CELL_DEV * LON_DEV + within % LON_DEV)


def taper_weight(source_ids, target_ids, circle):
    source_row, source_col = locate(source_ids)
    target_row, target_col = locate(target_ids)
    apart_cols = jnp.abs(source_col[:, None] - target_col[None, :])
    apart_cols = jnp.minimum(apart_cols, circle - apart_cols)
    apart_rows = source_row[:, None] - target_row[None, :]
    square = (apart_cols * apart_cols + apart_rows * apart_rows).astype(jnp.float32)
    return jnp.exp(square * (-2.0 / (LON_DEV * LON_DEV)))


def gain_parts(sample_now, observed, noise):
    centre = jnp.mean(sample_now, axis=0)
    spread = sample_now - centre
    covariance = jnp.dot(spread.T, spread, precision=highest) / (MEM - 1) + jnp.diag(noise)
    factor = jnp.linalg.cholesky(covariance)
    innovation = (observed - centre)[:, None]
    halfway = lax.linalg.triangular_solve(factor, innovation, left_side=True, lower=True)
    kalman_gain = lax.linalg.triangular_solve(
        factor, halfway, left_side=True, lower=True, transpose_a=True
    )[:, 0]
    rooted = factor + jnp.diag(jnp.sqrt(noise))
    identity = jnp.eye(OBS, dtype=noise.dtype)
    within = lax.linalg.triangular_solve(rooted, identity, left_side=True, lower=True)
    reduced = lax.linalg.triangular_solve(
        factor, within, left_side=True, lower=True, transpose_a=True
    )
    return (spread, kalman_gain, reduced)


def update_block(block, spread, kalman_gain, reduced, chosen, usable, obs_ids, local_ids, circle):
    levels = block.shape[1]
    rows_used = chosen.shape[0]
    weight = taper_weight(obs_ids[chosen], local_ids, circle) * usable[:, None]
    centre = jnp.mean(block, axis=0)
    flattened = (block - centre).reshape(MEM, -1)
    crossed = jnp.dot(spread[:, chosen].T, flattened, precision=highest) / (MEM - 1)
    tapered = (crossed.reshape(rows_used, levels, -1) * weight[:, None, :]).reshape(rows_used, -1)
    shifted = jnp.dot(kalman_gain[chosen], tapered, precision=highest)
    mixing = jnp.dot(spread, reduced[chosen].T, precision=highest)
    flattened = flattened - jnp.dot(mixing, tapered, precision=highest)
    return ((centre.reshape(-1) + shifted)[None, :] + flattened).reshape(block.shape)


def correct(upcoming, next_ids, now_ids, spread, kalman_gain, reduced, listed, circle, numbers):
    owners = next_ids // CELL_DEV
    lists_rows = listed.reshape(-1, ROUTE_CAP)[owners]
    member = jnp.any(lists_rows[:, :, None] == numbers[None, None, :], axis=1)
    weight = taper_weight(now_ids, next_ids, circle) * member.T.astype(jnp.float32)
    centre = jnp.mean(upcoming, axis=0)
    departure = upcoming - centre
    crossed = jnp.dot(spread.T, departure, precision=highest) / (MEM - 1)
    tapered = crossed * weight
    shifted = jnp.dot(kalman_gain, tapered, precision=highest)
    mixing = jnp.dot(spread, reduced.T, precision=highest)
    return (centre + shifted)[None, :] + departure - jnp.dot(mixing, tapered, precision=highest)


def body(ensemble, obs_cell, obs_value, obs_noise, obs_weight, tile_lists, batch_order):
    cell_table = collect(obs_cell, LON, 1)
    observed, noise = rows_first((obs_value, obs_noise), LON, (1, 1))
    tile_index = lax.axis_index(LON)
    circle = LON_DEV * lax.axis_size(LON)
    offset = tile_index * CELL_DEV
    local_ids = offset + jnp.arange(CELL_DEV, dtype=jnp.int32)
    numbers = jnp.arange(OBS, dtype=jnp.int32)

    def portion_of(block, current):
        cell_ids = cell_table[current]
        owned = ((cell_ids >= offset) & (cell_ids < offset + CELL_DEV)).astype(jnp.float32)
        within = jnp.clip(cell_ids - offset, 0, CELL_DEV - 1)
        picked = jnp.take(block, within, axis=2)
        return jnp.sum(picked * (obs_weight[current] * owned[None, :])[None], axis=1)

    def advance(block, sample_now, current):
        spread, kalman_gain, reduced = gain_parts(sample_now, observed[current], noise[current])
        listed = tile_lists[current]
        chosen = jnp.minimum(listed, OBS - 1)
        usable = (listed < OBS).astype(jnp.float32)
        block = update_block(
            block,
            spread,
            kalman_gain,
            reduced,
            chosen,
            usable,
            cell_table[current],
            local_ids,
            circle,
        )
        return (block, spread, kalman_gain, reduced)

    every_lists = collect(tile_lists, LON, 1)
    block_ids = jnp.arange(BATCHES, dtype=jnp.int32)
    portions = jax.vmap(lambda which: portion_of(ensemble, which))(block_ids)
    probes = sum_in_two_steps(portions, LON_LEV, (0, 1, 2, 3))

    def serial_turn(position, carried):
        block, probes = carried
        current = batch_order[position]
        block, spread, kalman_gain, reduced = advance(block, probes[current], current)

        def renew(upcoming, next_ids):
            return correct(
                upcoming,
                next_ids,
                cell_table[current],
                spread,
                kalman_gain,
                reduced,
                every_lists[current],
                circle,
                numbers,
            )

        probes = jax.vmap(renew)(probes, cell_table)
        return (block, probes)

    carried = (ensemble, probes)

    def grouped(groups, carried):
        for repeat in range(4):
            carried = serial_turn(4 * groups + repeat, carried)
        return carried

    finished = lax.fori_loop(0, BATCHES // 4, grouped, carried)
    return finished[0]


def solution(mesh):
    finer = Mesh(
        mesh.devices.reshape(4, 4, 4, mesh.shape["lev"]), ("lon_0", "lon_1", "lon_2", "lev")
    )
    in_specs = (
        P(None, "lev", LON),
        P(None, LON),
        P(None, LON),
        P(None, LON),
        P(None, "lev", None),
        P(None, LON),
        P(),
    )
    out_specs = P(None, "lev", LON)
    return jax.shard_map(body, mesh=finer, in_specs=in_specs, out_specs=out_specs, check_vma=False)
```

profile of v0, /device:TPU:1, one launch (start us, length us, event | category | flops | bytes accessed | tf_op | source)
XLA Modules:
  0.0 1259.0 jit_solution(5236757452238059833)
XLA Ops:
  9.0 12.0 all-to-all-start
  53.7 11.3 reduce-scatter.4.cloned.1.call-done
  65.2 147.6 %all-gather = f32[64,2,24]{2,1,0:T(2,128)S(1)} all-gather(f32[1,2,24]{2,1,0:T(2,128)S(1)} %maximum_bitcast_fusion), channel_id=1, replica_groups=mesh['lon_0'=4,'lon_1'=4,'lon_2'=4,'lev'=2] {'lon_0','lon_1','lon_2'}, dimensions={0}, use_global_device_ids=true | all-gather | bytes 12480 | tf_op jit(solution)/shard_map/all_gather | solution.py:39
  220.3 33.8 %reduce-scatter.8.cloned.1.call-done = f32[2,8,128]{2,1,0:T(8,128)} async-done(((f32[8,8,128]{2,1,0:T(8,128)}), f32[2,8,128]{2,1,0:T(8,128)}) %reduce-scatter.8.cloned.1.call-update) | async-done | bytes 8208 | tf_op jit(solution)/shard_map/reduce_scatter | solution.py:59
  280.1 10.7 all_gather.18
  292.7 958.0 %while.22 = (s32[]{:T(128)}, f32[80,8,1024]{2,1,0:T(8,128)S(1)}, f32[12,80,128]{2,1,0:T(8,128)}, s32[12]{0:T(128)S(1)}, f32[12,128]{1,0:T(8,128)S(1)}, /*index=5...) while((s32[]{:T(128)}, f32[80,8,1024]{2,1,0:T(8,128)S(1)}, ...), condition=%wide.region_24.30_spmd.clone.clone.clone, body=%wide.region_5.29_spmd.clone.clone.clone.sunk | while | flops 3445664256 | bytes 143802704 | solution.py:210
  303.8 11.7 cholesky.398
  362.4 11.7 cholesky.399
  420.2 12.5 cholesky.400
  485.7 13.2 %cholesky.401 = f32[128,128]{1,0:T(8,128)} custom-call(f32[128,128]{1,0:T(8,128)} %copy.185), custom_call_target="Cholesky" | custom-call | tf_op jit(solution)/shard_map/while/body/eval_jaxpr/jit(cholesky)/cholesky | solution.py:100
  502.5 11.3 custom-call.142
  515.5 11.3 custom-call.143
  622.7 11.7 cholesky.398
  681.4 11.7 cholesky.399
  739.2 12.5 cholesky.400
  804.6 13.2 %cholesky.401 = f32[128,128]{1,0:T(8,128)} custom-call(f32[128,128]{1,0:T(8,128)} %copy.185), custom_call_target="Cholesky" | custom-call | tf_op jit(solution)/shard_map/while/body/eval_jaxpr/jit(cholesky)/cholesky | solution.py:100
  821.4 11.3 custom-call.142
  834.4 11.3 custom-call.143
  941.7 11.7 cholesky.398
  1000.3 11.7 cholesky.399
  1058.1 12.5 cholesky.400
  1123.6 13.2 %cholesky.401 = f32[128,128]{1,0:T(8,128)} custom-call(f32[128,128]{1,0:T(8,128)} %copy.185), custom_call_target="Cholesky" | custom-call | tf_op jit(solution)/shard_map/while/body/eval_jaxpr/jit(cholesky)/cholesky | solution.py:100
  1140.3 11.3 custom-call.142
  1153.3 11.3 custom-call.143
  (1008 shorter events, 784.7 us)
Async XLA Ops:
  9.0 20.4 %all-to-all-start = ((s32[64,12,2]{1,2,0:T(2,128)}), s32[64,12,2]{1,2,0:T(2,128)S(1)}, u32[]{:S(2)}, u32[]{:S(2)}) async-start(s32[64,12,2]{1,2,0:T(2,128)} %broadcast_in_dim.481), calls=%async_computation | async-start | bytes 131072 | tf_op jit(solution)/shard_map/all_to_all | solution.py:28
  20.9 44.1 %reduce-scatter.4.cloned.1.call-start = ((), (), s32[]{:S(2)}) async-start(), calls=%async_computation.5 | async-start | bytes 655360 | tf_op jit(solution)/shard_map/reduce_scatter | solution.py:59
  44.9 168.7 %copy-start.74 = (u32[128]{0:T(128)S(1)}, u32[128]{0:T(128)}, u32[]{:S(2)}) copy-start(u32[128]{0:T(128)} %constant.1140) | copy-start | bytes 1540
  44.9 169.4 %copy-start.32 = (s32[64,12,2]{1,2,0:T(2,128)S(1)}, s32[64,12,2]{1,2,0:T(2,128)}, u32[]{:S(2)}) copy-start(s32[64,12,2]{1,2,0:T(2,128)} %copy-done.31) | copy-start | bytes 18436
  48.2 167.7 %all-to-all-start.1 = ((s32[64,1,288]{2,1,0:T(1,128)}), s32[64,1,288]{2,1,0:T(1,128)S(1)}, u32[]{:S(2)}, u32[]{:S(2)}) async-start(s32[64,1,288]{2,1,0:T(1,128)} %reshape.2419), calls=%async_computation.4 | async-start | bytes 196608 | tf_op jit(solution)/shard_map/all_to_all | solution.py:28
  53.6 160.6 %reduce-scatter.6.cloned.1.call-start = ((), (), s32[]{:S(2)}) async-start(), calls=%async_computation.6 | async-start | bytes 163840 | tf_op jit(solution)/shard_map/reduce_scatter | solution.py:59
  65.0 189.1 %reduce-scatter.8.cloned.1.call-start = ((), (), s32[]{:S(2)}) async-start(), calls=%async_computation.7 | async-start | bytes 40960 | tf_op jit(solution)/shard_map/reduce_scatter | solution.py:59
  214.2 78.4 %copy-start.44 = (s32[12]{0:T(128)S(1)}, s32[12]{0:T(128)}, u32[]{:S(2)}) copy-start(s32[12]{0:T(128)} %param.24) | copy-start | bytes 148
  293.2 60.5 %copy-start.38 = (s32[12,1,128]{2,0,1:T(8,128)}, s32[12,1,128]{2,0,1:T(8,128)S(1)}, u32[]{:S(2)}) copy-start(s32[12,1,128]{2,0,1:T(8,128)S(1)} %get-tuple-element.1268) | copy-start | bytes 18436 | tf_op jit(solution)/shard_map/while
  293.2 61.3 %copy-start.26 = (s32[12,128]{1,0:T(8,128)}, s32[12,128]{1,0:T(8,128)S(1)}, u32[]{:S(2)}) copy-start(s32[12,128]{1,0:T(8,128)S(1)} %get-tuple-element.1264) | copy-start | bytes 18436 | tf_op jit(solution)/shard_map/while
  361.7 50.6 %copy-start.10 = (f32[12,80,128]{2,1,0:T(8,128)}, f32[12,80,128]{2,1,0:T(8,128)S(1)}, u32[]{:S(2)}) copy-start(f32[12,80,128]{2,1,0:T(8,128)S(1)} %get-tuple-element.1124) | copy-start | bytes 1474564 | tf_op jit(solution)/shard_map/while
  417.4 55.3 %copy-start.9 = (f32[12,80,128]{2,1,0:T(8,128)}, f32[12,80,128]{2,1,0:T(8,128)S(1)}, u32[]{:S(2)}) copy-start(f32[12,80,128]{2,1,0:T(8,128)S(1)} %get-tuple-element.1135) | copy-start | bytes 1474564 | tf_op jit(solution)/shard_map/while
  474.6 53.8 %copy-start.54 = (s32[12,24]{1,0:T(8,128)S(1)}, s32[12,24]{1,0:T(8,128)}, u32[]{:S(2)}) copy-start(s32[12,24]{1,0:T(8,128)} %get-tuple-element.1263) | copy-start | bytes 3460 | tf_op jit(solution)/shard_map/while
  477.9 58.7 %copy-start.7 = (f32[12,80,128]{2,1,0:T(8,128)}, f32[12,80,128]{2,1,0:T(8,128)S(1)}, u32[]{:S(2)}) copy-start(f32[12,80,128]{2,1,0:T(8,128)S(1)} %get-tuple-element.1150) | copy-start | bytes 1474564 | tf_op jit(solution)/shard_map/while
  612.1 60.5 %copy-start.38 = (s32[12,1,128]{2,0,1:T(8,128)}, s32[12,1,128]{2,0,1:T(8,128)S(1)}, u32[]{:S(2)}) copy-start(s32[12,1,128]{2,0,1:T(8,128)S(1)} %get-tuple-element.1268) | copy-start | bytes 18436 | tf_op jit(solution)/shard_map/while
  612.1 61.3 %copy-start.26 = (s32[12,128]{1,0:T(8,128)}, s32[12,128]{1,0:T(8,128)S(1)}, u32[]{:S(2)}) copy-start(s32[12,128]{1,0:T(8,128)S(1)} %get-tuple-element.1264) | copy-start | bytes 18436 | tf_op jit(solution)/shard_map/while
  736.3 55.3 %copy-start.9 = (f32[12,80,128]{2,1,0:T(8,128)}, f32[12,80,128]{2,1,0:T(8,128)S(1)}, u32[]{:S(2)}) copy-start(f32[12,80,128]{2,1,0:T(8,128)S(1)} %get-tuple-element.1135) | copy-start | bytes 1474564 | tf_op jit(solution)/shard_map/while
  793.5 53.8 %copy-start.54 = (s32[12,24]{1,0:T(8,128)S(1)}, s32[12,24]{1,0:T(8,128)}, u32[]{:S(2)}) copy-start(s32[12,24]{1,0:T(8,128)} %get-tuple-element.1263) | copy-start | bytes 3460 | tf_op jit(solution)/shard_map/while
  796.8 58.7 %copy-start.7 = (f32[12,80,128]{2,1,0:T(8,128)}, f32[12,80,128]{2,1,0:T(8,128)S(1)}, u32[]{:S(2)}) copy-start(f32[12,80,128]{2,1,0:T(8,128)S(1)} %get-tuple-element.1150) | copy-start | bytes 1474564 | tf_op jit(solution)/shard_map/while
  931.0 60.5 %copy-start.38 = (s32[12,1,128]{2,0,1:T(8,128)}, s32[12,1,128]{2,0,1:T(8,128)S(1)}, u32[]{:S(2)}) copy-start(s32[12,1,128]{2,0,1:T(8,128)S(1)} %get-tuple-element.1268) | copy-start | bytes 18436 | tf_op jit(solution)/shard_map/while
  931.1 61.2 %copy-start.26 = (s32[12,128]{1,0:T(8,128)}, s32[12,128]{1,0:T(8,128)S(1)}, u32[]{:S(2)}) copy-start(s32[12,128]{1,0:T(8,128)S(1)} %get-tuple-element.1264) | copy-start | bytes 18436 | tf_op jit(solution)/shard_map/while
  1055.2 55.3 %copy-start.9 = (f32[12,80,128]{2,1,0:T(8,128)}, f32[12,80,128]{2,1,0:T(8,128)S(1)}, u32[]{:S(2)}) copy-start(f32[12,80,128]{2,1,0:T(8,128)S(1)} %get-tuple-element.1135) | copy-start | bytes 1474564 | tf_op jit(solution)/shard_map/while
  1112.4 53.8 %copy-start.54 = (s32[12,24]{1,0:T(8,128)S(1)}, s32[12,24]{1,0:T(8,128)}, u32[]{:S(2)}) copy-start(s32[12,24]{1,0:T(8,128)} %get-tuple-element.1263) | copy-start | bytes 3460 | tf_op jit(solution)/shard_map/while
  1115.7 58.7 %copy-start.7 = (f32[12,80,128]{2,1,0:T(8,128)}, f32[12,80,128]{2,1,0:T(8,128)S(1)}, u32[]{:S(2)}) copy-start(f32[12,80,128]{2,1,0:T(8,128)S(1)} %get-tuple-element.1150) | copy-start | bytes 1474564 | tf_op jit(solution)/shard_map/while
  (186 other events, 2202.8 us)
Sparse Core Ops, SparseCore 0:
  47.3 17.6 reduce-scatter.3
  67.4 19.4 reduce-scatter.5
  214.3 39.7 reduce-scatter.7
where the time goes:
time: 1280 us; the launch traced here: 1260 us
  other arithmetic  590 us (46%)
  local copies, waits for them, and re-layouts  201 us (16%)
  blocking collectives  184 us (14%)
  matrix products  174 us (14%)
  waiting for transfers between devices  49.6 us (4%)
  loops' own time  30.2 us (2%)
  starting transfers between devices  17.5 us (1%)
  between operations  13.6 us (1%)
    another operation x36, other arithmetic, gain_parts(): factor = jnp.linalg.cholesky(covariance)  158 us
    all_gather x1, blocking collectives, rows_first(): result = lax.all_gather(both, axis, axis=0, tiled=True)  148 us
    another operation x24, other arithmetic, gain_parts(): lax.linalg.triangular_solve(factor, halfway, left_side=True, lower=True,...  139 us
    reduce_or x12, other arithmetic, correct(): member = jnp.any(lists_rows[:, :, None] == numbers[None, None, :], axis=1)  125 us
    another operation x12, other arithmetic, gain_parts(): lax.linalg.triangular_solve(rooted, identity, left_side=True, lower=True)  122 us
    gather x12, local copies, waits for them, and re-layouts, correct(): lists_rows = listed.reshape(-1, ROUTE_CAP)[owners]  47.9 us
    dot_general x12, matrix products, update_block(): flattened = flattened - jnp.dot(mixing, tapered, precision=highest)  47.2 us
    reduce_scatter x3, waiting for transfers between devices, own_block(): parts = lax.psum_scatter(parts, axes[k], scatter_dimension=0, tiled=True)  45.1 us
  transfers between devices with their start and end apart: 5, of which 3 were waited for; matrix products, arithmetic and copies ran while one was open for 1% of the time, Pallas kernels for 0%

commit v1 on v0

v1 whole, which is shorter than its diff:
```python
import jax
import jax.numpy as jnp
from jax import lax
from jax.experimental import pallas as pl
from jax.experimental.pallas import tpu as pltpu
from jax.sharding import Mesh
from jax.sharding import PartitionSpec as P

MEM = 80
OBS = 128
ROUTE_CAP = 24
OWN_MAX = 8
LON_DEV = 16
CELL_DEV = 1024
BATCHES = 12
LEV_DEV = 8
ROWS = 32
LON = ("lon_0", "lon_1", "lon_2")
f32 = jnp.float32
bf16 = jnp.bfloat16


def sent_to_all(array, axis):
    copies = jnp.broadcast_to(array, (lax.axis_size(axis), *array.shape))
    return lax.all_to_all(copies, axis, split_axis=0, concat_axis=0, tiled=True)


def iota(shape, dim):
    return lax.broadcasted_iota(jnp.int32, shape, dim)


def split(x):
    high = x.astype(bf16)
    return high, (x - high.astype(f32)).astype(bf16)


def dot(a, b):
    return jnp.dot(a, b, preferred_element_type=f32)


def dot_lanes(a, b):
    return lax.dot_general(a, b, (((1,), (1,)), ((), ())), preferred_element_type=f32)


def lane_of(x, lane):
    return jnp.broadcast_to(x[:, lane : lane + 1], x.shape)


def sub_of(x, row):
    return jnp.broadcast_to(x[row : row + 1, :], x.shape)


def probe_kernel(tile_ref, ens_ref, table_ref, weight_ref, out_ref, turn_ref):
    tile = tile_ref[0]
    cells = table_ref[0:16, :].astype(jnp.int32)
    own = (cells >> 10) == tile
    lane = iota((OBS, OBS), 1)
    sub = iota((OBS, OBS), 0)
    before = (sub < lane).astype(f32).astype(bf16)
    rank = dot(own.astype(f32).astype(bf16), before)
    slot = jnp.where(own, iota((16, OBS), 0).astype(f32) * OWN_MAX + rank, -1.0)
    turn_ref[...] = jnp.zeros((OBS, OBS), f32)
    turn_ref[0:16, :] = slot
    slot_turned = turn_ref[...].T
    within = cells & (CELL_DEV - 1)
    row = (within >> 4).astype(f32)
    col = (within & 15).astype(f32)
    lane_f = lane.astype(f32)
    sub8 = iota((8, OBS), 0)
    picked = jnp.zeros((32, OBS), f32)
    for b in range(BATCHES):
        chosen = (lane_of(slot_turned, b) == lane_f).astype(f32).astype(bf16)
        weight = weight_ref[b]
        w_high = weight.astype(bf16).astype(f32)
        w_rest = weight - w_high
        w_mid = w_rest.astype(bf16).astype(f32)
        place = jnp.where(
            sub8 == 0,
            jnp.broadcast_to(row[b : b + 1, :], (8, OBS)),
            jnp.where(sub8 == 1, jnp.broadcast_to(col[b : b + 1, :], (8, OBS)), 0.0),
        )
        left = jnp.concatenate([place, w_high, w_mid, w_rest - w_mid], axis=0).astype(bf16)
        picked = picked + dot(left, chosen)
    cell = picked[0:1, :] * LON_DEV + picked[1:2, :]
    weight = picked[8:16, :] + picked[16:24, :] + picked[24:32, :]
    column = iota((CELL_DEV, OBS), 0).astype(f32)
    one_hot = (column == cell).astype(f32).astype(bf16)
    high, low = split(ens_ref[...])
    taken = dot(high, one_hot) + dot(low, one_hot)
    summed = jnp.sum(taken.reshape(MEM, LEV_DEV, OBS) * weight[None], axis=1)
    turn_ref[...] = jnp.zeros((OBS, OBS), f32)
    turn_ref[0:MEM, :] = summed
    out_ref[...] = turn_ref[...].T[0 : BATCHES * OWN_MAX, :]


def sweep(covariance, right, root):
    blocks = OBS // 8
    left_rows = [covariance[8 * i : 8 * i + 8, :] for i in range(blocks)]
    right_rows = [right[8 * i : 8 * i + 8, :] for i in range(blocks)]
    root_rows = [root[8 * i : 8 * i + 8, :] for i in range(blocks)]
    sub = iota((8, OBS), 0)
    for p in range(blocks):
        a, b, d = left_rows[p], right_rows[p], root_rows[p]
        columns = [lane_of(a, 8 * p + r) for r in range(8)]
        for j in range(8):
            pivot = sub_of(columns[j], j)
            inverse = 1.0 / pivot
            scale = 1.0 / (pivot + sub_of(d, j) * jnp.sqrt(pivot))
            at_j = sub == j
            row_a = sub_of(a, j) * inverse
            row_b = sub_of(b, j) * scale
            a = jnp.where(at_j, row_a, a - columns[j] * row_a)
            b = jnp.where(at_j, row_b, b - columns[j] * row_b)
            for r in range(j + 1, 8):
                row_c = sub_of(columns[r], j) * inverse
                columns[r] = jnp.where(at_j, row_c, columns[r] - columns[j] * row_c)
        left_rows[p], right_rows[p] = a, b
        rows_a = [sub_of(a, r) for r in range(8)]
        rows_b = [sub_of(b, r) for r in range(8)]
        for step in range(1, blocks):
            i = (p + step) % blocks
            old = left_rows[i]
            new_a, new_b = old, right_rows[i]
            for r in range(8):
                factor = lane_of(old, 8 * p + r)
                new_a = new_a - factor * rows_a[r]
                new_b = new_b - factor * rows_b[r]
            left_rows[i], right_rows[i] = new_a, new_b
    return jnp.concatenate(right_rows, axis=0)


def taper(rows_a, cols_a, rows_b, cols_b, circle):
    apart = jnp.abs(cols_a - cols_b)
    apart = jnp.minimum(apart, circle - apart)
    down = rows_a - rows_b
    return jnp.exp((apart * apart + down * down) * (-2.0 / (LON_DEV * LON_DEV)))


def serial_kernel(
    tiles,
    order_ref,
    tile_ref,
    probes_ref,
    table_ref,
    lists_ref,
    ens_ref,
    out_ref,
    raw_ref,
    state_ref,
    turn_ref,
    turn2_ref,
    rows_ref,
    paug_ref,
    row_ref,
    col_ref,
    tile_col_ref,
    value_ref,
    root_ref,
    noise_ref,
    listed_ref,
    weight_ref,
    sem,
):
    circle = float(LON_DEV * tiles)
    pieces = CELL_DEV // OBS

    def columns_of(ref, c):
        return ref.at[:, OBS * c : OBS * c + OBS]

    fetches = [pltpu.make_async_copy(columns_of(ens_ref, c), raw_ref.at[c], sem.at[c]) for c in range(pieces)]
    for fetch in fetches:
        fetch.start()
    square = (OBS, OBS)
    lane = iota(square, 1)
    sub = iota(square, 0)
    lane_f = lane.astype(f32)
    is_member = lane < MEM
    turn_ref[...] = jnp.zeros(square, f32)
    turn2_ref[...] = jnp.full(square, float(OBS), f32)
    for k in range(BATCHES):
        b = order_ref[k]
        for part in range(3):
            turn_ref[16 * part + k : 16 * part + k + 1, :] = table_ref[pl.ds(BATCHES * part + b, 1), :]
        turn2_ref[k : k + 1, 0:ROUTE_CAP] = lists_ref[pl.ds(b, 1), :]
    turned = turn_ref[...].T
    listed = turn2_ref[...].T
    cells = turn_ref[0:16, :].astype(jnp.int32)
    rows_ref[0] = ((cells & (CELL_DEV - 1)) >> 4).astype(f32)
    rows_ref[1] = ((cells >> 10) * LON_DEV + (cells & 15)).astype(f32)
    rows_ref[2] = (cells >> 10).astype(f32)
    ones = jnp.ones(square, f32).astype(bf16)
    for k in range(BATCHES):
        b = order_ref[k]
        cell = lane_of(turned, k).astype(jnp.int32)
        tile_col = (cell >> 10).astype(f32)
        row_ref[k] = ((cell & (CELL_DEV - 1)) >> 4).astype(f32)
        col_ref[k] = ((cell >> 10) * LON_DEV + (cell & 15)).astype(f32)
        tile_col_ref[k] = tile_col
        same = (tile_col == rows_ref[2, k : k + 1, :]) & (lane < sub)
        rank = dot(same.astype(f32).astype(bf16), ones)
        slot = tile_col * OWN_MAX + rank
        wide = tiles * OWN_MAX
        high, low = split(probes_ref[:, b].reshape(wide, OBS))
        gathered = jnp.zeros(square, f32)
        for c in range(wide // OBS):
            chosen = (slot == lane_f + float(OBS * c)).astype(f32).astype(bf16)
            part = slice(OBS * c, OBS * c + OBS)
            gathered = gathered + dot(chosen, high[part]) + dot(chosen, low[part])
        mean = jnp.sum(gathered, axis=1, keepdims=True) * (1.0 / MEM)
        mean = jnp.broadcast_to(mean, square)
        paug_ref[k] = jnp.where(is_member, gathered - mean, jnp.where(lane == MEM, mean, 0.0))
        value_ref[k] = lane_of(turned, 16 + k)
        noise = lane_of(turned, 32 + k)
        noise_ref[k] = jnp.where(lane == sub, noise, 0.0)
        root_ref[k] = jnp.where(is_member, jnp.sqrt(noise), 0.0)
        list_col = jnp.broadcast_to(listed[0:ROWS, k : k + 1], (ROWS, OBS))
        listed_ref[k] = (list_col == lane_f[0:ROWS]).astype(f32)
    for fetch in fetches:
        fetch.wait()
    for c in range(pieces):
        for level in range(LEV_DEV):
            state_ref[level, :, OBS * c : OBS * c + OBS] = raw_ref[c, pl.ds(level, MEM, stride=LEV_DEV), :]
    first_col = (tile_ref[0] * LON_DEV).astype(f32)
    here = iota((ROWS, CELL_DEV), 1)
    here_row = (here >> 4).astype(f32)
    here_col = (here & 15).astype(f32) + first_col

    def turn(k, carry):
        now = paug_ref[k]
        spread = jnp.where(is_member, now, 0.0)
        high, low = split(spread)
        covariance = dot_lanes(high, high) + dot_lanes(low, high) + dot_lanes(high, low)
        covariance = covariance * (1.0 / (MEM - 1)) + noise_ref[k]
        right = jnp.where(is_member, now, jnp.where(lane == MEM, value_ref[k] - now, 0.0))
        solved = sweep(covariance, right, root_ref[k])
        push = jnp.where(is_member, -solved, solved)
        push_high, push_low = split(push)

        source_row = rows_ref[0, pl.ds(k, 1), :]
        source_col = rows_ref[1, pl.ds(k, 1), :]
        source_tile = rows_ref[2, pl.ds(k, 1), :]

        def renew(other, carry):
            upcoming = paug_ref[other]
            up_high, up_low = split(jnp.where(is_member, upcoming, 0.0))
            crossed = dot_lanes(up_high, high) + dot_lanes(up_low, high) + dot_lanes(up_high, low)
            apart = jnp.abs(tile_col_ref[other] - source_tile)
            near = (apart <= 1.0) | (apart >= float(tiles - 1))
            weight = taper(row_ref[other], col_ref[other], source_row, source_col, circle)
            tapered = crossed * jnp.where(near, weight * (1.0 / (MEM - 1)), 0.0)
            t_high, t_low = split(tapered)
            change = dot(t_high, push_high) + dot(t_low, push_high) + dot(t_high, push_low)
            paug_ref[other] = upcoming + change
            return carry

        lax.fori_loop(k + 1, BATCHES, renew, 0)

        chosen_f = listed_ref[k]
        chosen = chosen_f.astype(bf16)
        s_high = dot(chosen, high)
        s_low = dot(chosen, low)
        lane_s = lane[0:ROWS]
        moved = pltpu.roll(s_high, MEM, 1)
        first = jnp.where(lane_s < MEM, s_high, moved)
        second = jnp.where(lane_s < 2 * MEM - OBS, moved, pltpu.roll(s_low, 2 * MEM - OBS, 1))
        left = jnp.concatenate([first, second], axis=1).astype(bf16)
        gain = dot(chosen, push_high) + dot(chosen, push_low)
        gain = jnp.where(lane_s < MEM, gain + lane_of(gain, MEM), 0.0)
        gain_high = gain.astype(bf16).astype(f32)
        stacked = jnp.concatenate([gain_high, gain_high, gain - gain_high, jnp.zeros_like(gain)], axis=0)
        mixing = stacked.T[0:MEM, :].astype(bf16)
        row_of = jnp.sum(chosen_f * source_row, axis=1, keepdims=True)
        col_of = jnp.sum(chosen_f * source_col, axis=1, keepdims=True)
        weight_ref[...] = taper(row_of, col_of, here_row, here_col, circle) * (1.0 / (MEM - 1))

        def renew_level(level, carry):
            block = state_ref[level]
            x_high, x_low = split(block)
            filler = jnp.zeros((16, CELL_DEV), bf16)
            crossed = dot(left, jnp.concatenate([x_high, x_low, x_high, filler], axis=0))
            tapered = crossed * weight_ref[...]
            t_high, t_low = split(tapered)
            filler = jnp.zeros((ROWS, CELL_DEV), bf16)
            change = dot(mixing, jnp.concatenate([t_high, t_low, t_high, filler], axis=0))
            state_ref[level] = block + change
            return carry

        lax.fori_loop(0, LEV_DEV, renew_level, 0)
        return carry

    lax.fori_loop(0, BATCHES, turn, 0)
    stores = [pltpu.make_async_copy(raw_ref.at[c], columns_of(out_ref, c), sem.at[c]) for c in range(pieces)]
    for c in range(pieces):
        for level in range(LEV_DEV):
            raw_ref[c, pl.ds(level, MEM, stride=LEV_DEV), :] = state_ref[level, :, OBS * c : OBS * c + OBS]
        stores[c].start()
    for store in stores:
        store.wait()


def whole(space):
    return pl.BlockSpec(memory_space=space)


def body(ensemble, obs_cell, obs_value, obs_noise, obs_weight, tile_lists, batch_order):
    tiles = lax.axis_size(LON)
    tile = jnp.reshape(lax.axis_index(LON), (1,)).astype(jnp.int32)
    mine = jnp.concatenate([obs_cell.astype(f32), obs_value, obs_noise], axis=0)
    table = sent_to_all(mine, LON)
    table = jnp.moveaxis(table, 0, 1).reshape(3 * BATCHES, OBS)
    flat = ensemble.reshape(MEM * LEV_DEV, CELL_DEV)
    slots = BATCHES * OWN_MAX
    portion = pl.pallas_call(
        probe_kernel,
        name="probe_kernel",
        out_shape=jax.ShapeDtypeStruct((slots, OBS), f32),
        in_specs=[whole(pltpu.SMEM), whole(pltpu.VMEM), whole(pltpu.VMEM), whole(pltpu.VMEM)],
        out_specs=whole(pltpu.VMEM),
        scratch_shapes=[pltpu.VMEM((OBS, OBS), f32)],
        compiler_params=pltpu.CompilerParams(vmem_limit_bytes=32 << 20),
    )(tile, flat, table, obs_weight)
    portion = lax.psum(portion, "lev")
    probes = sent_to_all(portion, LON).reshape(tiles, BATCHES, OWN_MAX, OBS)
    square = (BATCHES, OBS, OBS)

    def run(*refs):
        serial_kernel(tiles, *refs)

    result = pl.pallas_call(
        run,
        name="serial_kernel",
        out_shape=jax.ShapeDtypeStruct(flat.shape, f32),
        in_specs=[
            whole(pltpu.SMEM),
            whole(pltpu.SMEM),
            whole(pltpu.VMEM),
            whole(pltpu.VMEM),
            whole(pltpu.VMEM),
            whole(pl.ANY),
        ],
        out_specs=whole(pl.ANY),
        scratch_shapes=[
            pltpu.VMEM((CELL_DEV // OBS, MEM * LEV_DEV, OBS), f32),
            pltpu.VMEM((LEV_DEV, MEM, CELL_DEV), f32),
            pltpu.VMEM((OBS, OBS), f32),
            pltpu.VMEM((OBS, OBS), f32),
            pltpu.VMEM((3, 16, OBS), f32),
            pltpu.VMEM(square, f32),
            pltpu.VMEM(square, f32),
            pltpu.VMEM(square, f32),
            pltpu.VMEM(square, f32),
            pltpu.VMEM(square, f32),
            pltpu.VMEM(square, f32),
            pltpu.VMEM(square, f32),
            pltpu.VMEM((BATCHES, ROWS, OBS), f32),
            pltpu.VMEM((ROWS, CELL_DEV), f32),
            pltpu.SemaphoreType.DMA((CELL_DEV // OBS,)),
        ],
        compiler_params=pltpu.CompilerParams(vmem_limit_bytes=48 << 20),
    )(batch_order, tile, probes, table, tile_lists.astype(f32), flat)
    return result.reshape(MEM, LEV_DEV, CELL_DEV)


def solution(mesh):
    finer = Mesh(
        mesh.devices.reshape(4, 4, 4, mesh.shape["lev"]), ("lon_0", "lon_1", "lon_2", "lev")
    )
    in_specs = (
        P(None, "lev", LON),
        P(None, LON),
        P(None, LON),
        P(None, LON),
        P(None, "lev", None),
        P(None, LON),
        P(),
    )
    out_specs = P(None, "lev", LON)
    return jax.shard_map(body, mesh=finer, in_specs=in_specs, out_specs=out_specs, check_vma=False)
```

time: 1280 us -> 200 us (0.16); the launches traced: 1260 us -> 198 us
  other arithmetic: 590 us -> 1.45 us
  local copies, waits for them, and re-layouts: 201 us -> 7.05 us
  blocking collectives: 184 us -> 5.45 us
  matrix products: 174 us -> 0 us
  Pallas kernels: 0 us -> 119 us
  loops' own time: 30.2 us -> 0 us
  between operations: 13.6 us -> 0.06 us
    another operation x72 -> x0, other arithmetic: 419 us -> none  [the longest x36 158 us: gain_parts(): factor = jnp.linalg.cholesky(covariance)]
    all_gather x5 -> x0, blocking collectives: 178 us -> none  [the longest x1 148 us: rows_first(): result = lax.all_gather(both, axis, axis=0, tiled=True)]
    dot_general x108 -> x0, matrix products: 147 us -> none  [the longest x12 47.2 us: update_block(): flattened = flattened - jnp.dot(mixing, tapered, precision=highest)]
    reduce_or x12 -> x0, other arithmetic: 125 us -> none  [correct(): member = jnp.any(lists_rows[:, :, None] == numbers[None, None, :], axis=1)]
    pallas_call x0 -> x2, Pallas kernels: none -> 119 us  [the longest x1 117 us: body(): pl.pallas_call(run, name='serial_kernel', out_shape=jax.ShapeDtypeStruct(...]
    gather x63 -> x0, local copies, waits for them, and re-layouts: 103 us -> none  [the longest x12 47.9 us: correct(): lists_rows = listed.reshape(-1, ROUTE_CAP)[owners]]
    reduce_scatter x3 -> x0, waiting for transfers between devices: 45.1 us -> none  [own_block(): parts = lax.psum_scatter(parts, axes[k], scatter_dimension=0, tiled=True)]
    all_to_all x2, waiting for transfers between devices: 4.39 us -> 48.6 us  [sent_to_all(): return lax.all_to_all(copies, axis, split_axis=0, concat_axis=0, tiled=True)]
  transfers between devices with their start and end apart: 5 -> 2, of which waited for: 3 -> 2; matrix products, arithmetic and copies ran while one was open for 1% -> 0% of each run, Pallas kernels for 0% -> 0%
where the time goes in v1:
time: 200 us; the launch traced here: 198 us
  Pallas kernels  119 us (60%)
  waiting for transfers between devices  48.6 us (24%)
  starting transfers between devices  16.8 us (8%)
  local copies, waits for them, and re-layouts  7.05 us (4%)
  blocking collectives  5.45 us (3%)
    pallas_call x1, Pallas kernels, body(): pl.pallas_call(run, name='serial_kernel', out_shape=jax.ShapeDtypeStruct(...  117 us
    all_to_all x2, waiting for transfers between devices, sent_to_all(): return lax.all_to_all(copies, axis, split_axis=0, concat_axis=0, tiled=True)  48.6 us
    all_to_all x2, starting transfers between devices, sent_to_all(): return lax.all_to_all(copies, axis, split_axis=0, concat_axis=0, tiled=True)  16.8 us
    psum x1, blocking collectives, body(): portion = lax.psum(portion, 'lev')  5.45 us
    unnamed x10, local copies, waits for them, and re-layouts  4.3 us
  transfers between devices with their start and end apart: 2, of which 2 were waited for; matrix products, arithmetic and copies ran while one was open for 0% of the time, Pallas kernels for 0%

profile of v1, /device:TPU:1, one launch (start us, length us, event | category | flops | bytes accessed | tf_op | source)
XLA Modules:
  0.0 198.5 jit_solution(2393156090556628447)
XLA Ops:
  0.0 0.7 convert_element_type.6
  0.7 0.8 pad_maximum_fusion
  1.5 0.7 broadcast_in_dim.6
  2.1 12.0 %all-to-all-start = ((f32[64,36,2]{1,2,0:T(2,128)}), f32[64,36,2]{1,2,0:T(2,128)S(1)}, u32[]{:S(2)}, u32[]{:S(2)}) async-start(f32[64,36,2]{1,2,0:T(2,128)} %broadcast_in_dim.6), calls=%async_computation | async-start | bytes 131072 | tf_op jit(solution)/shard_map/all_to_all | solution.py:25
  14.1 8.4 %all-to-all-done = f32[64,36,2]{1,2,0:T(2,128)S(1)} async-done(((f32[64,36,2]{1,2,0:T(2,128)}), f32[64,36,2]{1,2,0:T(2,128)S(1)}, u32[]{:S(2)}, u32[]{:S(2)}) %all-to-all-start) | async-done | bytes 18464 | tf_op jit(solution)/shard_map/all_to_all | solution.py:25
  22.5 0.1 copy.9.table_ref.refs_3_
  22.6 0.0 copy-start
  22.6 1.8 copy-done
  24.3 0.0 copy-start.2
  24.3 0.8 copy-done.2
  25.1 1.7 probe_kernel.1
  26.8 5.4 %psum.7 = f32[96,128]{1,0:T(8,128)S(1)} all-reduce(f32[96,128]{1,0:T(8,128)S(1)} %probe_kernel.1), channel_id=1, replica_groups=mesh['lon_0'=4,'lon_1'=4,'lon_2'=4,'lev'=2] {'lev'}, use_global_device_ids=true, to_apply=%region_0.0 | all-reduce | flops 12288 | bytes 98304 | tf_op jit(solution)/shard_map/psum | solution.py:322
  32.3 2.0 %broadcast_in_dim.7 = f32[64,96,128]{2,1,0:T(8,128)} broadcast(f32[96,128]{1,0:T(8,128)S(1)} %psum.7), dimensions={1,2} | broadcast | bytes 3194880 | tf_op jit(solution)/shard_map/broadcast_in_dim | solution.py:24
  34.3 0.0 copy-start.4
  34.3 0.0 copy-start.3
  34.3 4.9 %all-to-all-start.1 = ((f32[64,96,128]{2,1,0:T(8,128)}), f32[64,96,128]{2,1,0:T(8,128)S(1)}, u32[]{:S(2)}, u32[]{:S(2)}) async-start(f32[64,96,128]{2,1,0:T(8,128)} %broadcast_in_dim.7), calls=%async_computation.1 | async-start | bytes 6291456 | tf_op jit(solution)/shard_map/all_to_all | solution.py:25
  39.2 0.0 copy-done.4
  39.2 40.2 %all-to-all-done.1 = f32[64,96,128]{2,1,0:T(8,128)S(1)} async-done(((f32[64,96,128]{2,1,0:T(8,128)}), f32[64,96,128]{2,1,0:T(8,128)S(1)}, u32[]{:S(2)}, u32[]{:S(2)}) %all-to-all-start.1) | async-done | bytes 3145760 | tf_op jit(solution)/shard_map/all_to_all | solution.py:25
  79.4 0.0 copy-done.3
  79.4 0.0 copy-start.1
  79.4 1.7 copy-done.1
  81.1 117.3 %serial_kernel.1 = f32[640,1024]{1,0:T(8,128)} custom-call(s32[12]{0:T(128)S(1)} %copy-done.3, s32[1]{0:T(128)} %bitcast.tile_ref.refs_1_, f32[64,12,8,128]{3,2,1,0:T(8,128)S(1)} %bitcast.7, f32[36,128]{1,0:T(8,128)S(1)} %copy.9.table_ref.refs_3_, f32[12,24]{1,0:T(8,128)S(1)} %convert_element_type.7.refs_4_, f32[640,1024]{1,0:T(8,128)S(1)} %bitcast.9), custom_call_target="tpu_custom_call" | custom-call | tf_op jit(solution)/shard_map/serial_kernel/pallas_call | solution.py:329
  (1 shorter events, 0.0 us)
Async XLA Ops:
  2.1 20.4 %all-to-all-start = ((f32[64,36,2]{1,2,0:T(2,128)}), f32[64,36,2]{1,2,0:T(2,128)S(1)}, u32[]{:S(2)}, u32[]{:S(2)}) async-start(f32[64,36,2]{1,2,0:T(2,128)} %broadcast_in_dim.6), calls=%async_computation | async-start | bytes 131072 | tf_op jit(solution)/shard_map/all_to_all | solution.py:25
  22.6 1.8 copy-start
  24.3 0.8 copy-start.2
  34.3 4.9 %copy-start.4 = (s32[12,24]{1,0:T(8,128)S(1)}, s32[12,24]{1,0:T(8,128)}, u32[]{:S(2)}) copy-start(s32[12,24]{1,0:T(8,128)} %param.12) | copy-start | bytes 3460
  34.3 45.1 %copy-start.3 = (s32[12]{0:T(128)S(1)}, s32[12]{0:T(128)}, u32[]{:S(2)}) copy-start(s32[12]{0:T(128)} %refs_0_.1) | copy-start | bytes 148
  34.3 45.1 %all-to-all-start.1 = ((f32[64,96,128]{2,1,0:T(8,128)}), f32[64,96,128]{2,1,0:T(8,128)S(1)}, u32[]{:S(2)}, u32[]{:S(2)}) async-start(f32[64,96,128]{2,1,0:T(8,128)} %broadcast_in_dim.7), calls=%async_computation.1 | async-start | bytes 6291456 | tf_op jit(solution)/shard_map/all_to_all | solution.py:25
  79.4 1.7 copy-start.1

commit v2 on v1

v2 whole, which is shorter than its diff:
```python
import jax
import jax.numpy as jnp
from jax import lax
from jax.experimental import pallas as pl
from jax.experimental.pallas import tpu as pltpu
from jax.sharding import Mesh
from jax.sharding import PartitionSpec as P

MEM = 80
OBS = 128
ROUTE_CAP = 24
OWN_MAX = 8
LON_DEV = 16
CELL_DEV = 1024
BATCHES = 12
LEV_DEV = 8
ROWS = 32
HALF = 6
PACK = 32
SEGMENT = 12
LON = ("lon_0", "lon_1", "lon_2")
f32 = jnp.float32
bf16 = jnp.bfloat16


def sent_to_all(array, axis):
    copies = jnp.broadcast_to(array, (lax.axis_size(axis), *array.shape))
    return lax.all_to_all(copies, axis, split_axis=0, concat_axis=0, tiled=True)


def iota(shape, dim):
    return lax.broadcasted_iota(jnp.int32, shape, dim)


def split(x):
    high = x.astype(bf16)
    return high, (x - high.astype(f32)).astype(bf16)


def dot(a, b):
    return jnp.dot(a, b, preferred_element_type=f32)


def dot_lanes(a, b):
    return lax.dot_general(a, b, (((1,), (1,)), ((), ())), preferred_element_type=f32)


def lane_of(x, lane):
    return jnp.broadcast_to(x[:, lane : lane + 1], x.shape)


def sub_of(x, row):
    return jnp.broadcast_to(x[row : row + 1, :], x.shape)


def probe_kernel(place_ref, ens_ref, table_ref, weight_ref, keep_ref, send_ref, turn_ref, block_ref, sem):
    tile, level_half = place_ref[0], place_ref[1]
    fetch = pltpu.make_async_copy(ens_ref, block_ref, sem)
    fetch.start()
    cells = table_ref[0:16, :].astype(jnp.int32)
    own = (cells >> 10) == tile
    lane = iota((OBS, OBS), 1)
    sub = iota((OBS, OBS), 0)
    before = (sub < lane).astype(f32).astype(bf16)
    rank = dot(own.astype(f32).astype(bf16), before)
    slot = jnp.where(own, iota((16, OBS), 0).astype(f32) * OWN_MAX + rank, -1.0)
    turn_ref[...] = jnp.zeros((OBS, OBS), f32)
    turn_ref[0:16, :] = slot
    slot_turned = turn_ref[...].T
    within = cells & (CELL_DEV - 1)
    row = (within >> 4).astype(f32)
    col = (within & 15).astype(f32)
    lane_f = lane.astype(f32)
    sub8 = iota((8, OBS), 0)
    picked = jnp.zeros((32, OBS), f32)
    for b in range(BATCHES):
        chosen = (lane_of(slot_turned, b) == lane_f).astype(f32).astype(bf16)
        weight = weight_ref[b]
        w_high = weight.astype(bf16).astype(f32)
        w_rest = weight - w_high
        w_mid = w_rest.astype(bf16).astype(f32)
        place = jnp.where(
            sub8 == 0,
            jnp.broadcast_to(row[b : b + 1, :], (8, OBS)),
            jnp.where(sub8 == 1, jnp.broadcast_to(col[b : b + 1, :], (8, OBS)), 0.0),
        )
        left = jnp.concatenate([place, w_high, w_mid, w_rest - w_mid], axis=0).astype(bf16)
        picked = picked + dot(left, chosen)
    cell = picked[0:1, :] * LON_DEV + picked[1:2, :]
    weight = picked[8:16, :] + picked[16:24, :] + picked[24:32, :]
    column = iota((CELL_DEV, OBS), 0).astype(f32)
    one_hot = (column == cell).astype(f32).astype(bf16)
    fetch.wait()
    high, low = split(block_ref[...])
    taken = dot(high, one_hot) + dot(low, one_hot)
    summed = jnp.sum(taken.reshape(MEM, LEV_DEV, OBS) * weight[None], axis=1)
    turn_ref[...] = jnp.zeros((OBS, OBS), f32)
    turn_ref[0:MEM, :] = summed
    turn_ref[...] = turn_ref[...].T
    lane6 = iota((HALF, OBS), 1)
    for half, out_ref in ((level_half, keep_ref), (1 - level_half, send_ref)):
        first = half * (HALF * OWN_MAX)
        slots = [turn_ref[pl.ds(first + s, HALF, stride=OWN_MAX), :] for s in range(OWN_MAX)]
        out_ref[...] = jnp.zeros((PACK, OBS), f32)
        tail = jnp.zeros((HALF, OBS), f32)
        for r in range(4):
            both = jnp.where(lane6 < 64, slots[r], pltpu.roll(slots[r + 4], 64, 1))
            out_ref[HALF * r : HALF * r + HALF, :] = both
        for s in range(OWN_MAX):
            tail = jnp.where((lane6 >> 4) == s, pltpu.roll(slots[s], (16 * s + 64) % OBS, 1), tail)
        out_ref[HALF * 4 : HALF * 5, :] = tail


def sweep(covariance, right, root, fill):
    blocks = OBS // 8
    left_rows = [covariance[8 * i : 8 * i + 8, :] for i in range(blocks)]
    right_rows = [right[8 * i : 8 * i + 8, :] for i in range(blocks)]
    root_rows = [root[8 * i : 8 * i + 8, :] for i in range(blocks)]
    sub = iota((8, OBS), 0)
    for p in range(blocks):
        a, b, d = left_rows[p], right_rows[p], root_rows[p]
        columns = [lane_of(a, 8 * p + r) for r in range(8)]
        scale = jnp.ones((8, OBS), f32)
        for j in range(8):
            at_j = sub == j
            pivot = sub_of(columns[j], j)
            inverse = 1.0 / pivot
            others = jnp.where(at_j, 0.0, columns[j])
            factor = others * inverse
            if j < 7:
                ahead = others * sub_of(columns[j + 1], j)
                columns[j + 1] = columns[j + 1] - ahead * inverse
            for r in range(j + 2, 8):
                columns[r] = columns[r] - factor * sub_of(columns[r], j)
            a = a - factor * sub_of(a, j)
            b = b * jnp.where(at_j, 1.0 / (1.0 + sub_of(d, j) * lax.rsqrt(pivot)), 1.0)
            b = b - factor * sub_of(b, j)
            scale = jnp.where(at_j, inverse, scale)
        a, b = a * scale, b * scale
        left_rows[p], right_rows[p] = a, b
        rows_a = [sub_of(a, r) for r in range(8)]
        rows_b = [sub_of(b, r) for r in range(8)]
        for step in range(1, blocks):
            i = (p + step) % blocks
            old = left_rows[i]
            new_a, new_b = old, right_rows[i]
            for r in range(8):
                factor = lane_of(old, 8 * p + r)
                if p < blocks - 1:
                    new_a = new_a - factor * rows_a[r]
                new_b = new_b - factor * rows_b[r]
            left_rows[i], right_rows[i] = new_a, new_b
        fill(p)
    return jnp.concatenate(right_rows, axis=0)


def covariance_of(spread):
    high = spread.astype(bf16)
    rest = spread - high.astype(f32)
    mid = rest.astype(bf16)
    low = (rest - mid.astype(f32)).astype(bf16)
    small = dot_lanes(high, low) + dot_lanes(low, high) + dot_lanes(mid, mid)
    return dot_lanes(high, high) + (dot_lanes(high, mid) + dot_lanes(mid, high) + small)


def taper(rows_a, cols_a, rows_b, cols_b, circle):
    apart = jnp.abs(cols_a - cols_b)
    apart = jnp.minimum(apart, circle - apart)
    down = rows_a - rows_b
    return jnp.exp((apart * apart + down * down) * (-2.0 / (LON_DEV * LON_DEV)))


def pair_index(k, other):
    return k * (2 * BATCHES - 1 - k) // 2 + other - k - 1


def index_kernel(
    tiles,
    order_ref,
    place_ref,
    after_ref,
    table_ref,
    lists_ref,
    ens_ref,
    state_ref,
    pair_ref,
    local_ref,
    listed_ref,
    rank_ref,
    tile_col_ref,
    value_ref,
    root_ref,
    noise_ref,
    token_ref,
    raw_ref,
    turn_ref,
    turn2_ref,
    rows_ref,
    row_ref,
    col_ref,
    sem,
):
    circle = float(LON_DEV * tiles)
    pieces = CELL_DEV // OBS
    fetches = [
        pltpu.make_async_copy(ens_ref.at[:, OBS * c : OBS * c + OBS], raw_ref.at[c], sem.at[c])
        for c in range(pieces)
    ]
    for fetch in fetches:
        fetch.start()
    token_ref[...] = jnp.zeros((8, OBS), f32)
    listed_ref[BATCHES] = jnp.zeros((ROWS, OBS), f32)
    square = (OBS, OBS)
    lane = iota(square, 1)
    sub = iota(square, 0)
    lane_f = lane.astype(f32)
    turn_ref[...] = jnp.zeros(square, f32)
    turn2_ref[...] = jnp.full(square, float(OBS), f32)
    for k in range(BATCHES):
        b = order_ref[k]
        for part in range(3):
            turn_ref[16 * part + k : 16 * part + k + 1, :] = table_ref[pl.ds(BATCHES * part + b, 1), :]
        turn2_ref[k : k + 1, 0:ROUTE_CAP] = lists_ref[pl.ds(b, 1), :].astype(f32)
    turned = turn_ref[...].T
    listed = turn2_ref[...].T
    cells = turn_ref[0:16, :].astype(jnp.int32)
    rows_ref[0] = ((cells & (CELL_DEV - 1)) >> 4).astype(f32)
    rows_ref[1] = ((cells >> 10) * LON_DEV + (cells & 15)).astype(f32)
    rows_ref[2] = (cells >> 10).astype(f32)
    ones = jnp.ones(square, f32).astype(bf16)
    first_col = (place_ref[0] * LON_DEV).astype(f32)
    here = iota((ROWS, CELL_DEV), 1)
    here_row = (here >> 4).astype(f32)
    here_col = (here & 15).astype(f32) + first_col
    for k in range(BATCHES):
        cell = lane_of(turned, k).astype(jnp.int32)
        tile_col = (cell >> 10).astype(f32)
        row_ref[k] = ((cell & (CELL_DEV - 1)) >> 4).astype(f32)
        col_ref[k] = ((cell >> 10) * LON_DEV + (cell & 15)).astype(f32)
        tile_col_ref[k] = tile_col
        same = (tile_col == rows_ref[2, k : k + 1, :]) & (lane < sub)
        rank_ref[k] = dot(same.astype(f32).astype(bf16), ones)
        value_ref[k] = lane_of(turned, 16 + k)
        noise = lane_of(turned, 32 + k)
        noise_ref[k] = jnp.where(lane == sub, noise, 0.0)
        root_ref[k] = jnp.where(lane < MEM, jnp.sqrt(noise), 0.0)
        list_col = jnp.broadcast_to(listed[0:ROWS, k : k + 1], (ROWS, OBS))
        chosen = (list_col == lane_f[0:ROWS]).astype(f32)
        listed_ref[k] = chosen
        row_of = jnp.sum(chosen * rows_ref[0, k : k + 1, :], axis=1, keepdims=True)
        col_of = jnp.sum(chosen * rows_ref[1, k : k + 1, :], axis=1, keepdims=True)
        local_ref[k] = taper(row_of, col_of, here_row, here_col, circle) * (1.0 / (MEM - 1))

    def pairs(k, carry):
        source_row = rows_ref[0, pl.ds(k, 1), :]
        source_col = rows_ref[1, pl.ds(k, 1), :]
        source_tile = rows_ref[2, pl.ds(k, 1), :]

        def pair(other, carry):
            apart = jnp.abs(tile_col_ref[other] - source_tile)
            near = (apart <= 1.0) | (apart >= float(tiles - 1))
            weight = taper(row_ref[other], col_ref[other], source_row, source_col, circle)
            pair_ref[pair_index(k, other)] = jnp.where(near, weight * (1.0 / (MEM - 1)), 0.0)
            return carry

        return lax.fori_loop(k + 1, BATCHES, pair, carry)

    lax.fori_loop(0, BATCHES, pairs, 0)
    for fetch in fetches:
        fetch.wait()
    for c in range(pieces):
        for level in range(LEV_DEV):
            state_ref[level, :, OBS * c : OBS * c + OBS] = raw_ref[c, pl.ds(level, MEM, stride=LEV_DEV), :]


def serial_kernel(
    tiles,
    order_ref,
    place_ref,
    mine_ref,
    other_ref,
    token_ref,
    state_sent,
    pair_sent,
    local_sent,
    listed_sent,
    rank_sent,
    tile_col_sent,
    value_sent,
    root_sent,
    noise_sent,
    out_ref,
    state_ref,
    pair_ref,
    local_ref,
    listed_ref,
    rank_ref,
    tile_col_ref,
    value_ref,
    root_ref,
    noise_ref,
    raw_ref,
    paug_ref,
    past_ref,
    sem,
    sent_sem,
):
    moves = (
        (tile_col_sent, tile_col_ref),
        (rank_sent, rank_ref),
        (noise_sent, noise_ref),
        (value_sent, value_ref),
        (root_sent, root_ref),
        (listed_sent, listed_ref),
        (local_sent, local_ref),
        (pair_sent, pair_ref),
        (state_sent, state_ref),
    )
    fetches = [pltpu.make_async_copy(a, b, sent_sem.at[n]) for n, (a, b) in enumerate(moves)]
    for fetch in fetches:
        fetch.start()
    for fetch in fetches[:2]:
        fetch.wait()
    pieces = CELL_DEV // OBS
    square = (OBS, OBS)
    lane = iota(square, 1)
    lane_f = lane.astype(f32)
    is_member = lane < MEM
    group = lane >> 4
    fold = (lane == 64 + (iota(square, 0) & 15)).astype(f32).astype(bf16)
    lane_t = lane_f[:, 0:tiles]
    for k in range(BATCHES):
        b = order_ref[k]
        half = b // HALF
        here = b - half * HALF
        from_mine = half == place_ref[1]
        rank = rank_ref[k].astype(jnp.int32)
        chosen = (tile_col_ref[k, :, 0:tiles] == lane_t).astype(f32).astype(bf16)
        sent = []
        for r in range(5):
            rows = pl.ds(HALF * r + here, tiles, stride=PACK)
            sent.extend(split(jnp.where(from_mine, mine_ref[rows, :], other_ref[rows, :])))
        taken = dot(chosen, jnp.concatenate(sent, axis=1))
        parts = [taken[:, OBS * c : OBS * c + OBS] for c in range(10)]
        body = parts[0] + parts[1]
        for r in range(1, 4):
            body = jnp.where((rank & 3) == r, parts[2 * r] + parts[2 * r + 1], body)
        body = jnp.where(rank >= 4, pltpu.roll(body, 64, 1), body)
        at_rank = group == rank
        tail = dot(jnp.where(at_rank, parts[8], 0.0).astype(bf16), fold)
        tail = tail + dot(jnp.where(at_rank, parts[9], 0.0).astype(bf16), fold)
        gathered = jnp.where(lane < 64, body, tail)
        gathered = jnp.where(is_member, gathered, 0.0)
        mean = jnp.sum(gathered, axis=1, keepdims=True) * (1.0 / MEM)
        mean = jnp.broadcast_to(mean, square)
        paug_ref[k] = jnp.where(is_member, gathered - mean, jnp.where(lane == MEM, mean, 0.0))
    for fetch in fetches[2:]:
        fetch.wait()

    is_member_s = is_member[0:ROWS]
    lane_s = lane[0:ROWS]
    last_pair = pair_ref.shape[0] - 1
    for extra in range(BATCHES, 2 * BATCHES):
        paug_ref[extra] = jnp.zeros(square, f32)
    for part in range(4):
        past_ref[part] = jnp.zeros(square, bf16)

    def operators():
        high, low, push_high, push_low = (past_ref[part] for part in range(4))
        chosen = listed_ref[BATCHES].astype(bf16)
        s_high = dot(chosen, high)
        s_low = dot(chosen, low)
        moved = pltpu.roll(s_high, MEM, 1)
        first = jnp.where(is_member_s, s_high, moved)
        second = jnp.where(lane_s < 2 * MEM - OBS, moved, pltpu.roll(s_low, 2 * MEM - OBS, 1))
        left = jnp.concatenate([first, second], axis=1).astype(bf16)
        gain = dot(chosen, push_high) + dot(chosen, push_low)
        gain = jnp.where(is_member_s, gain + lane_of(gain, MEM), 0.0)
        gain_high = gain.astype(bf16).astype(f32)
        stacked = jnp.concatenate([gain_high, gain_high, gain - gain_high, jnp.zeros_like(gain)], axis=0)
        return left, stacked.T[0:MEM, :].astype(bf16)

    def renew_level(level, before, left, mixing):
        block = state_ref[level]
        x_high, x_low = split(block)
        filler = jnp.zeros((16, CELL_DEV), bf16)
        crossed = dot(left, jnp.concatenate([x_high, x_low, x_high, filler], axis=0))
        tapered = crossed * local_ref[before]
        t_high, t_low = split(tapered)
        filler = jnp.zeros((ROWS, CELL_DEV), bf16)
        change = dot(mixing, jnp.concatenate([t_high, t_low, t_high, filler], axis=0))
        state_ref[level] = block + change

    def tapered_by(upcoming, high, low, pair):
        up_high, up_low = split(jnp.where(is_member, upcoming, 0.0))
        crossed = dot_lanes(up_high, high) + dot_lanes(up_low, high) + dot_lanes(up_high, low)
        return split(crossed * pair_ref[jnp.clip(pair, 0, last_pair)])

    def pushed(parts, push_high, push_low):
        t_high, t_low = parts
        return dot(t_high, push_high) + dot(t_low, push_high) + dot(t_high, push_low)

    def turn(k, slots):
        before = jnp.maximum(k - 1, 0)
        now = paug_ref[k]
        spread = jnp.where(is_member, now, 0.0)
        high, low = split(spread)
        old_high, old_low, old_push_high, old_push_low = (past_ref[part] for part in range(4))
        left, mixing = operators()
        covariance = covariance_of(spread) * (1.0 / (MEM - 1)) + noise_ref[k]
        right = jnp.where(is_member, now, jnp.where(lane == MEM, value_ref[k] - now, 0.0))
        ready = []

        def fill(p):
            if p < slots:
                other = k + 1 + p
                upcoming = paug_ref[other]
                parts = tapered_by(upcoming, old_high, old_low, pair_index(k - 1, other))
                upcoming = upcoming + pushed(parts, old_push_high, old_push_low)
                paug_ref[other] = upcoming
                if p == 0:
                    ready.append(upcoming)
                    ready.append(tapered_by(upcoming, high, low, pair_index(k, other)))
            if p % 2 == 1:
                renew_level(p // 2, before, left, mixing)

        solved = sweep(covariance, right, root_ref[k], fill)
        push = jnp.where(is_member, -solved, solved)
        push_high, push_low = split(push)
        paug_ref[k + 1] = ready[0] + pushed(ready[1], push_high, push_low)
        for part, value in enumerate((high, low, push_high, push_low)):
            past_ref[part] = value
        listed_ref[BATCHES] = listed_ref[k]

    for start in range(0, BATCHES, SEGMENT):

        def step(k, carry):
            turn(k, BATCHES - 1 - start)
            return carry

        lax.fori_loop(start, start + SEGMENT, step, 0)
    left, mixing = operators()
    for level in range(LEV_DEV):
        renew_level(level, BATCHES - 1, left, mixing)
    stores = [
        pltpu.make_async_copy(raw_ref.at[c], out_ref.at[:, OBS * c : OBS * c + OBS], sem.at[c])
        for c in range(pieces)
    ]
    for c in range(pieces):
        for level in range(LEV_DEV):
            raw_ref[c, pl.ds(level, MEM, stride=LEV_DEV), :] = state_ref[level, :, OBS * c : OBS * c + OBS]
        stores[c].start()
    for store in stores:
        store.wait()


def whole(space):
    return pl.BlockSpec(memory_space=space)


def body(ensemble, obs_cell, obs_value, obs_noise, obs_weight, tile_lists, batch_order):
    tiles = lax.axis_size(LON)
    place = jnp.stack([lax.axis_index(LON), lax.axis_index("lev")]).astype(jnp.int32)
    mine = jnp.concatenate([obs_cell.astype(f32), obs_value, obs_noise], axis=0)
    table = sent_to_all(mine, LON)
    table = jnp.moveaxis(table, 0, 1).reshape(3 * BATCHES, OBS)
    flat = ensemble.reshape(MEM * LEV_DEV, CELL_DEV)
    packed = jax.ShapeDtypeStruct((PACK, OBS), f32)
    keep, send = pl.pallas_call(
        probe_kernel,
        name="probe_kernel",
        out_shape=(packed, packed),
        in_specs=[whole(pltpu.SMEM), whole(pl.ANY), whole(pltpu.VMEM), whole(pltpu.VMEM)],
        out_specs=(whole(pltpu.VMEM), whole(pltpu.VMEM)),
        scratch_shapes=[
            pltpu.VMEM((OBS, OBS), f32),
            pltpu.VMEM(flat.shape, f32),
            pltpu.SemaphoreType.DMA,
        ],
        compiler_params=pltpu.CompilerParams(vmem_limit_bytes=62 << 20),
    )(place, flat, table, obs_weight)
    swap = [(0, 1), (1, 0)]
    portion = keep + lax.ppermute(send, "lev", swap)
    mine = sent_to_all(portion, LON)
    square = (BATCHES, OBS, OBS)
    pair_count = BATCHES * (BATCHES - 1) // 2
    state_shape = (LEV_DEV, MEM, CELL_DEV)
    raw_shape = (CELL_DEV // OBS, MEM * LEV_DEV, OBS)

    def index_run(*refs):
        given, sent, token, held, rest = refs[:6], refs[6:15], refs[15], refs[16:25], refs[25:]
        index_kernel(tiles, *given, *held, token, *rest[:-1])
        copies = [pltpu.make_async_copy(a, b, rest[-1].at[n]) for n, (a, b) in enumerate(zip(held, sent))]
        for copy in copies:
            copy.start()
        for copy in copies:
            copy.wait()

    shapes = (
        state_shape,
        (pair_count, OBS, OBS),
        (BATCHES, ROWS, CELL_DEV),
        (BATCHES + 1, ROWS, OBS),
        square,
        square,
        square,
        square,
        square,
        (8, OBS),
    )
    known = pl.pallas_call(
        index_run,
        name="index_kernel",
        out_shape=tuple(jax.ShapeDtypeStruct(shape, f32) for shape in shapes),
        in_specs=[whole(pltpu.SMEM)] * 2 + [whole(pltpu.VMEM)] * 3 + [whole(pl.ANY)],
        out_specs=tuple(whole(pltpu.HBM) for shape in shapes[:-1]) + (whole(pltpu.VMEM),),
        scratch_shapes=[pltpu.VMEM(shape, f32) for shape in shapes[:-1]]
        + [
            pltpu.VMEM(raw_shape, f32),
            pltpu.VMEM((OBS, OBS), f32),
            pltpu.VMEM((OBS, OBS), f32),
            pltpu.VMEM((3, 16, OBS), f32),
            pltpu.VMEM(square, f32),
            pltpu.VMEM(square, f32),
            pltpu.SemaphoreType.DMA((CELL_DEV // OBS,)),
            pltpu.SemaphoreType.DMA((len(shapes) - 1,)),
        ],
        cost_estimate=pl.CostEstimate(flops=40 << 20, transcendentals=2 << 20, bytes_accessed=16 << 20),
        compiler_params=pltpu.CompilerParams(vmem_limit_bytes=62 << 20),
    )(batch_order, place, portion, table, tile_lists, flat)
    mine, token = lax.optimization_barrier((mine, known[-1]))
    known = (*known[:-1], token)
    other = lax.ppermute(mine, "lev", swap)
    mine = mine.reshape(tiles * PACK, OBS)
    other = other.reshape(tiles * PACK, OBS)

    def run(*refs):
        serial_kernel(tiles, *refs)

    result = pl.pallas_call(
        run,
        name="serial_kernel",
        out_shape=jax.ShapeDtypeStruct(flat.shape, f32),
        in_specs=[whole(pltpu.SMEM)] * 2
        + [whole(pltpu.VMEM)] * 3
        + [whole(pltpu.HBM)] * 9,
        out_specs=whole(pl.ANY),
        scratch_shapes=[pltpu.VMEM(shape, f32) for shape in shapes[:-1]]
        + [
            pltpu.VMEM(raw_shape, f32),
            pltpu.VMEM((2 * BATCHES, OBS, OBS), f32),
            pltpu.VMEM((4, OBS, OBS), bf16),
            pltpu.SemaphoreType.DMA((CELL_DEV // OBS,)),
            pltpu.SemaphoreType.DMA((len(shapes) - 1,)),
        ],
        compiler_params=pltpu.CompilerParams(vmem_limit_bytes=60 << 20),
    )(batch_order, place, mine, other, known[-1], *known[:-1])
    return result.reshape(MEM, LEV_DEV, CELL_DEV)


def solution(mesh):
    finer = Mesh(
        mesh.devices.reshape(4, 4, 4, mesh.shape["lev"]), ("lon_0", "lon_1", "lon_2", "lev")
    )
    in_specs = (
        P(None, "lev", LON),
        P(None, LON),
        P(None, LON),
        P(None, LON),
        P(None, "lev", None),
        P(None, LON),
        P(),
    )
    out_specs = P(None, "lev", LON)
    return jax.shard_map(body, mesh=finer, in_specs=in_specs, out_specs=out_specs, check_vma=False)
```

time: 200 us -> 133 us (0.67)
  waiting for transfers between devices: 48.6 us -> 16.6 us
  Pallas kernels: 119 us -> 88.4 us
  blocking collectives: 5.45 us -> 0 us
  starting transfers between devices: 16.8 us -> 20.8 us
  local copies, waits for them, and re-layouts: 7.05 us -> 3.42 us
    pallas_call x1, Pallas kernels: 117 us -> 71.8 us  [body(): pl.pallas_call(run, name='serial_kernel', out_shape=jax.ShapeDtypeStruct(...]
    all_to_all x2, waiting for transfers between devices: 48.6 us -> 13.3 us  [sent_to_all(): return lax.all_to_all(copies, axis, split_axis=0, concat_axis=0, tiled=True)]
    pallas_call x1 -> x2, Pallas kernels: 1.67 us -> 16.6 us  [the longest x1 12.3 us: body(): pl.pallas_call(index_run, name='index_kernel', out_shape=tuple((jax.Shape...]
    psum x1 -> x0, blocking collectives: 5.45 us -> none  [body(): portion = lax.psum(portion, 'lev')]
    ppermute x0 -> x2, starting transfers between devices: none -> 4.13 us  [the longest x1 2.19 us: body(): portion = keep + lax.ppermute(send, 'lev', swap)]
    ppermute x0 -> x2, waiting for transfers between devices: none -> 3.34 us  [the longest x1 2.29 us: body(): other = lax.ppermute(mine, 'lev', swap)]
    unnamed x10 -> x6, local copies, waits for them, and re-layouts: 4.3 us -> 0.99 us
  transfers between devices with their start and end apart: 2 -> 4, of which waited for: 2 -> 4; matrix products, arithmetic and copies ran while one was open for 0% -> 0% of each run, Pallas kernels for 0% -> 9%
where the time goes in v2:
time: 133 us; the launch traced here: 132 us
  Pallas kernels  88.4 us (66%)
  starting transfers between devices  20.8 us (16%)
  waiting for transfers between devices  16.6 us (12%)
  local copies, waits for them, and re-layouts  3.42 us (3%)
  other arithmetic  2.76 us (2%)
    pallas_call x1, Pallas kernels, body(): pl.pallas_call(run, name='serial_kernel', out_shape=jax.ShapeDtypeStruct(...  71.8 us
    all_to_all x2, starting transfers between devices, sent_to_all(): return lax.all_to_all(copies, axis, split_axis=0, concat_axis=0, tiled=True)  16.6 us
    all_to_all x2, waiting for transfers between devices, sent_to_all(): return lax.all_to_all(copies, axis, split_axis=0, concat_axis=0, tiled=True)  13.3 us
    pallas_call x1, Pallas kernels, body(): pl.pallas_call(index_run, name='index_kernel', out_shape=tuple((jax.Shape...  12.3 us
    pallas_call x1, Pallas kernels, body(): pl.pallas_call(probe_kernel, name='probe_kernel', out_shape=(packed, pack...  4.32 us
  transfers between devices with their start and end apart: 4, of which 4 were waited for; matrix products, arithmetic and copies ran while one was open for 0% of the time, Pallas kernels for 9%

profile of v2, /device:TPU:1, one launch (start us, length us, event | category | flops | bytes accessed | tf_op | source)
XLA Modules:
  0.0 132.2 jit_solution(2328700744761994894)
XLA Ops:
  0.0 0.7 convert_element_type.3
  0.7 0.8 pad_maximum_fusion
  1.5 0.7 broadcast_in_dim.6
  2.1 12.0 %all-to-all-start = ((f32[64,36,2]{1,2,0:T(2,128)}), f32[64,36,2]{1,2,0:T(2,128)S(1)}, u32[]{:S(2)}, u32[]{:S(2)}) async-start(f32[64,36,2]{1,2,0:T(2,128)} %broadcast_in_dim.6), calls=%async_computation | async-start | bytes 131072 | tf_op jit(solution)/shard_map/all_to_all | solution.py:28
  14.1 0.6 pad_add_fusion.place_ref.refs_1_
  14.7 7.8 %all-to-all-done = f32[64,36,2]{1,2,0:T(2,128)S(1)} async-done(((f32[64,36,2]{1,2,0:T(2,128)}), f32[64,36,2]{1,2,0:T(2,128)S(1)}, u32[]{:S(2)}, u32[]{:S(2)}) %all-to-all-start) | async-done | bytes 18464 | tf_op jit(solution)/shard_map/all_to_all | solution.py:28
  22.5 0.7 copy.9.table_ref.refs_3_
  23.2 4.3 %probe_kernel.1 = (f32[32,128]{1,0:T(8,128)}, f32[32,128]{1,0:T(8,128)}) custom-call(s32[2]{0:T(128)} %pad_add_fusion.place_ref.refs_1_, f32[640,1024]{1,0:T(8,128)} %bitcast.10, f32[36,128]{1,0:T(8,128)} %copy.9.table_ref.refs_3_, f32[12,8,128]{2,1,0:T(8,128)} %weight_ref.1), custom_call_target="tpu_custom_call" | custom-call | tf_op jit(solution)/shard_map/probe_kernel/pallas_call | solution.py:469
  27.5 2.2 %collective-permute-start = (f32[32,128]{1,0:T(8,128)}, f32[32,128]{1,0:T(8,128)S(1)}, u32[]{:S(2)}, u32[]{:S(2)}) collective-permute-start(f32[32,128]{1,0:T(8,128)} %get-tuple-element.20), channel_id=1, source_target_pairs={{0,1},{1,0},{2,3},{3,2},{4,5},{5,4},{6,7},{7,6},{8,9},{9,8},{10,11... | collective-permute-start | bytes 49160 | tf_op jit(solution)/shard_map/ppermute | solution.py:483
  29.7 1.0 collective-permute-done
  30.7 0.7 add.11.refs_2_
  31.5 0.0 copy-start.2
  31.5 1.1 broadcast_in_dim.7
  32.6 4.7 %all-to-all-start.1 = ((f32[64,32,128]{2,1,0:T(8,128)}), f32[64,32,128]{2,1,0:T(8,128)S(1)}, u32[]{:S(2)}, u32[]{:S(2)}) async-start(f32[64,32,128]{2,1,0:T(8,128)} %broadcast_in_dim.7), calls=%async_computation.1 | async-start | bytes 2097152 | tf_op jit(solution)/shard_map/all_to_all | solution.py:28
  37.3 0.0 copy-done.2
  37.3 12.3 %index_kernel.1 = (f32[8,80,1024]{2,1,0:T(8,128)}, f32[66,128,128]{2,1,0:T(8,128)}, f32[12,32,1024]{2,1,0:T(8,128)}, f32[13,32,128]{2,1,0:T(8,128)}, f32[12,128,...) custom-call(s32[12]{0:T(128)} %refs_0_.3, ...), custom_call_target="tpu_custom_call" | custom-call | flops 41943040 | bytes 16777216 | tf_op jit(solution)/shard_map/index_kernel/pallas_call | solution.py:511
  49.5 5.4 %all-to-all-done.1 = f32[64,32,128]{2,1,0:T(8,128)S(1)} async-done(((f32[64,32,128]{2,1,0:T(8,128)}), f32[64,32,128]{2,1,0:T(8,128)S(1)}, u32[]{:S(2)}, u32[]{:S(2)}) %all-to-all-start.1) | async-done | bytes 1048608 | tf_op jit(solution)/shard_map/all_to_all | solution.py:28
  55.0 0.0 copy-start
  55.0 1.9 %collective-permute-start.1 = (f32[64,32,128]{2,1,0:T(8,128)S(1)}, f32[64,32,128]{2,1,0:T(8,128)S(1)}, u32[]{:S(2)}, u32[]{:S(2)}) collective-permute-start(f32[64,32,128]{2,1,0:T(8,128)S(1)} %all-to-all-done.1), channel_id=1, source_target_pairs={{0,1},{1,0},{2,3},{3,2},{4,5},{5,4},{6,7},{7,6},{8,9},{9,8},{10,11... | collective-permute-start | bytes 3145736 | tf_op jit(solution)/shard_map/ppermute | solution.py:533
  56.9 2.3 %collective-permute-done.1 = f32[64,32,128]{2,1,0:T(8,128)S(1)} collective-permute-done((f32[64,32,128]{2,1,0:T(8,128)S(1)}, f32[64,32,128]{2,1,0:T(8,128)S(1)}, u32[]{:S(2)}, u32[]{:S(2)}) %collective-permute-start.1) | collective-permute-done | bytes 1048608 | tf_op jit(solution)/shard_map/ppermute | solution.py:533
  59.2 0.0 copy-start.1
  59.2 0.0 copy-done
  59.2 1.0 copy-done.1
  60.2 71.8 %serial_kernel.1 = f32[640,1024]{1,0:T(8,128)} custom-call(s32[12]{0:T(128)} %refs_0_.3, s32[2]{0:T(128)} %pad_add_fusion.place_ref.refs_1_, f32[2048,128]{1,0:T(8,128)} %bitcast.9, f32[2048,128]{1,0:T(8,128)} %bitcast.12, f32[8,128]{1,0:T(8,128)} %get-tuple-element.23.refs_4_, f32[8,80,1024]{2,1,0:T(8,128)} %get-tuple-element.24.refs_5_, ...), custom_call_target="tpu_custom_call" | custom-call | tf_op jit(solution)/shard_map/serial_kernel/pallas_call | solution.py:540
Async XLA Ops:
  2.1 20.4 %all-to-all-start = ((f32[64,36,2]{1,2,0:T(2,128)}), f32[64,36,2]{1,2,0:T(2,128)S(1)}, u32[]{:S(2)}, u32[]{:S(2)}) async-start(f32[64,36,2]{1,2,0:T(2,128)} %broadcast_in_dim.6), calls=%async_computation | async-start | bytes 131072 | tf_op jit(solution)/shard_map/all_to_all | solution.py:28
  27.5 3.2 %collective-permute-start = (f32[32,128]{1,0:T(8,128)}, f32[32,128]{1,0:T(8,128)S(1)}, u32[]{:S(2)}, u32[]{:S(2)}) collective-permute-start(f32[32,128]{1,0:T(8,128)} %get-tuple-element.20), channel_id=1, source_target_pairs={{0,1},{1,0},{2,3},{3,2},{4,5},{5,4},{6,7},{7,6},{8,9},{9,8},{10,11... | collective-permute-start | bytes 49160 | tf_op jit(solution)/shard_map/ppermute | solution.py:483
  31.5 5.8 %copy-start.2 = (f32[32,128]{1,0:T(8,128)}, f32[32,128]{1,0:T(8,128)S(1)}, u32[]{:S(2)}) copy-start(f32[32,128]{1,0:T(8,128)S(1)} %add.11.refs_2_) | copy-start | bytes 49156
  32.6 22.4 %all-to-all-start.1 = ((f32[64,32,128]{2,1,0:T(8,128)}), f32[64,32,128]{2,1,0:T(8,128)S(1)}, u32[]{:S(2)}, u32[]{:S(2)}) async-start(f32[64,32,128]{2,1,0:T(8,128)} %broadcast_in_dim.7), calls=%async_computation.1 | async-start | bytes 2097152 | tf_op jit(solution)/shard_map/all_to_all | solution.py:28
  55.0 4.2 %copy-start = (f32[64,32,128]{2,1,0:T(8,128)}, f32[64,32,128]{2,1,0:T(8,128)S(1)}, u32[]{:S(2)}) copy-start(f32[64,32,128]{2,1,0:T(8,128)S(1)} %all-to-all-done.1) | copy-start | bytes 3145732
  55.0 4.2 %collective-permute-start.1 = (f32[64,32,128]{2,1,0:T(8,128)S(1)}, f32[64,32,128]{2,1,0:T(8,128)S(1)}, u32[]{:S(2)}, u32[]{:S(2)}) collective-permute-start(f32[64,32,128]{2,1,0:T(8,128)S(1)} %all-to-all-done.1), channel_id=1, source_target_pairs={{0,1},{1,0},{2,3},{3,2},{4,5},{5,4},{6,7},{7,6},{8,9},{9,8},{10,11... | collective-permute-start | bytes 3145736 | tf_op jit(solution)/shard_map/ppermute | solution.py:533
  59.2 1.0 copy-start.1

commit v3 on v2

--- a/solution.py
+++ b/solution.py
@@ -17,7 +17,10 @@
 ROWS = 32
 HALF = 6
 PACK = 32
-SEGMENT = 12
+SEGMENT = 4
+LAG = 3
+WIDE = 16
+LEVEL_TURNS = (2, 4, 6, 8, 10, 11, 12, 13)
 LON = ("lon_0", "lon_1", "lon_2")
 f32 = jnp.float32
 bf16 = jnp.bfloat16
@@ -111,46 +114,88 @@
         out_ref[HALF * 4 : HALF * 5, :] = tail
 
 
+def split3(x):
+    high = x.astype(bf16)
+    rest = x - high.astype(f32)
+    mid = rest.astype(bf16)
+    return high, mid, (rest - mid.astype(f32)).astype(bf16)
+
+
+def product_of_panel(factors, rows, panel):
+    above, below = panel * WIDE, OBS - (panel + 1) * WIDE
+
+    def placed(part):
+        pieces = [part]
+        if above:
+            pieces.insert(0, jnp.zeros((above, OBS), bf16))
+        if below:
+            pieces.append(jnp.zeros((below, OBS), bf16))
+        return jnp.concatenate(pieces, axis=0)
+
+    high, mid, low = (placed(part) for part in split3(rows))
+    right = jnp.concatenate([high, high, high, mid, mid, low], axis=0)
+    return dot(factors, right)
+
+
 def sweep(covariance, right, root, fill):
     blocks = OBS // 8
+    deep = WIDE // 8
     left_rows = [covariance[8 * i : 8 * i + 8, :] for i in range(blocks)]
     right_rows = [right[8 * i : 8 * i + 8, :] for i in range(blocks)]
     root_rows = [root[8 * i : 8 * i + 8, :] for i in range(blocks)]
     sub = iota((8, OBS), 0)
-    for p in range(blocks):
-        a, b, d = left_rows[p], right_rows[p], root_rows[p]
-        columns = [lane_of(a, 8 * p + r) for r in range(8)]
-        scale = jnp.ones((8, OBS), f32)
-        for j in range(8):
-            at_j = sub == j
-            pivot = sub_of(columns[j], j)
+    for panel in range(OBS // WIDE):
+        own = range(deep * panel, deep * panel + deep)
+        near = range(own.stop, min(own.stop + deep, blocks))
+        base = WIDE * panel
+        a = [left_rows[i] for i in own]
+        b = [right_rows[i] for i in own]
+        d = [root_rows[i] for i in own]
+        columns = [[lane_of(a[h], base + r) for h in range(deep)] for r in range(WIDE)]
+        high, mid, low = split3(jnp.concatenate(left_rows, axis=0))
+        factors = jnp.concatenate([high, mid, low, high, mid, high], axis=1)
+        scale = [jnp.ones((8, OBS), f32) for h in range(deep)]
+        for j in range(WIDE):
+            block, at = divmod(j, 8)
+            at_j = sub == at
+            pivot = sub_of(columns[j][block], at)
             inverse = 1.0 / pivot
-            others = jnp.where(at_j, 0.0, columns[j])
-            factor = others * inverse
-            if j < 7:
-                ahead = others * sub_of(columns[j + 1], j)
-                columns[j + 1] = columns[j + 1] - ahead * inverse
-            for r in range(j + 2, 8):
-                columns[r] = columns[r] - factor * sub_of(columns[r], j)
-            a = a - factor * sub_of(a, j)
-            b = b * jnp.where(at_j, 1.0 / (1.0 + sub_of(d, j) * lax.rsqrt(pivot)), 1.0)
-            b = b - factor * sub_of(b, j)
-            scale = jnp.where(at_j, inverse, scale)
-        a, b = a * scale, b * scale
-        left_rows[p], right_rows[p] = a, b
-        rows_a = [sub_of(a, r) for r in range(8)]
-        rows_b = [sub_of(b, r) for r in range(8)]
-        for step in range(1, blocks):
-            i = (p + step) % blocks
+            others = list(columns[j])
+            others[block] = jnp.where(at_j, 0.0, others[block])
+            factor = [other * inverse for other in others]
+            if j + 1 < WIDE:
+                row = sub_of(columns[j + 1][block], at)
+                columns[j + 1] = [c - (o * row) * inverse for c, o in zip(columns[j + 1], others)]
+            for r in range(j + 2, WIDE):
+                row = sub_of(columns[r][block], at)
+                columns[r] = [c - f * row for c, f in zip(columns[r], factor)]
+            row = sub_of(a[block], at)
+            a = [x - f * row for x, f in zip(a, factor)]
+            weaker = 1.0 / (1.0 + sub_of(d[block], at) * lax.rsqrt(pivot))
+            b[block] = b[block] * jnp.where(at_j, weaker, 1.0)
+            row = sub_of(b[block], at)
+            b = [x - f * row for x, f in zip(b, factor)]
+            scale[block] = jnp.where(at_j, inverse, scale[block])
+        a = [x * s for x, s in zip(a, scale)]
+        b = [x * s for x, s in zip(b, scale)]
+        for i in near:
             old = left_rows[i]
-            new_a, new_b = old, right_rows[i]
-            for r in range(8):
-                factor = lane_of(old, 8 * p + r)
-                if p < blocks - 1:
-                    new_a = new_a - factor * rows_a[r]
-                new_b = new_b - factor * rows_b[r]
-            left_rows[i], right_rows[i] = new_a, new_b
-        fill(p)
+            for r in range(WIDE):
+                factor = lane_of(old, base + r)
+                left_rows[i] = left_rows[i] - factor * sub_of(a[r // 8], r % 8)
+                right_rows[i] = right_rows[i] - factor * sub_of(b[r // 8], r % 8)
+        far = [i for i in range(blocks) if i not in own and i not in near]
+        change = product_of_panel(factors, jnp.concatenate(b, axis=0), panel)
+        for i in far:
+            right_rows[i] = right_rows[i] - change[8 * i : 8 * i + 8, :]
+        if panel + 1 < OBS // WIDE:
+            change = product_of_panel(factors, jnp.concatenate(a, axis=0), panel)
+            for i in far:
+                left_rows[i] = left_rows[i] - change[8 * i : 8 * i + 8, :]
+        for h, i in enumerate(own):
+            left_rows[i], right_rows[i] = a[h], b[h]
+        for part in range(deep):
+            fill(deep * panel + part)
     return jnp.concatenate(right_rows, axis=0)
 
 
@@ -365,31 +410,31 @@
     for part in range(4):
         past_ref[part] = jnp.zeros(square, bf16)
 
-    def operators():
+    def select():
         high, low, push_high, push_low = (past_ref[part] for part in range(4))
         chosen = listed_ref[BATCHES].astype(bf16)
-        s_high = dot(chosen, high)
-        s_low = dot(chosen, low)
+        return dot(chosen, high), dot(chosen, low), dot(chosen, push_high) + dot(chosen, push_low)
+
+    def operators(s_high, s_low, gain):
         moved = pltpu.roll(s_high, MEM, 1)
         first = jnp.where(is_member_s, s_high, moved)
         second = jnp.where(lane_s < 2 * MEM - OBS, moved, pltpu.roll(s_low, 2 * MEM - OBS, 1))
         left = jnp.concatenate([first, second], axis=1).astype(bf16)
-        gain = dot(chosen, push_high) + dot(chosen, push_low)
         gain = jnp.where(is_member_s, gain + lane_of(gain, MEM), 0.0)
         gain_high = gain.astype(bf16).astype(f32)
         stacked = jnp.concatenate([gain_high, gain_high, gain - gain_high, jnp.zeros_like(gain)], axis=0)
         return left, stacked.T[0:MEM, :].astype(bf16)
 
-    def renew_level(level, before, left, mixing):
-        block = state_ref[level]
-        x_high, x_low = split(block)
+    def crossed_level(level, before, left):
+        x_high, x_low = split(state_ref[level])
         filler = jnp.zeros((16, CELL_DEV), bf16)
         crossed = dot(left, jnp.concatenate([x_high, x_low, x_high, filler], axis=0))
-        tapered = crossed * local_ref[before]
-        t_high, t_low = split(tapered)
+        t_high, t_low = split(crossed * local_ref[before])
         filler = jnp.zeros((ROWS, CELL_DEV), bf16)
-        change = dot(mixing, jnp.concatenate([t_high, t_low, t_high, filler], axis=0))
-        state_ref[level] = block + change
+        return jnp.concatenate([t_high, t_low, t_high, filler], axis=0)
+
+    def renew_level(level, mixing, tapered):
+        state_ref[level] = state_ref[level] + dot(mixing, tapered)
 
     def tapered_by(upcoming, high, low, pair):
         up_high, up_low = split(jnp.where(is_member, upcoming, 0.0))
@@ -406,28 +451,48 @@
         spread = jnp.where(is_member, now, 0.0)
         high, low = split(spread)
         old_high, old_low, old_push_high, old_push_low = (past_ref[part] for part in range(4))
-        left, mixing = operators()
         covariance = covariance_of(spread) * (1.0 / (MEM - 1)) + noise_ref[k]
         right = jnp.where(is_member, now, jnp.where(lane == MEM, value_ref[k] - now, 0.0))
-        ready = []
+        waiting = []
+        made = {}
+
+        def finish_slot(slot, other, parts):
+            upcoming = paug_ref[other] + pushed(parts, old_push_high, old_push_low)
+            if slot == 0:
+                made["next"] = upcoming
+
+                def taper_next():
+                    made["tapered"] = tapered_by(upcoming, high, low, pair_index(k, other))
+
+                waiting.append(taper_next)
+            else:
+                paug_ref[other] = upcoming
 
         def fill(p):
+            ready = waiting[:-LAG] if p < OBS // 8 - 1 else waiting[:]
+            del waiting[: len(ready)]
+            for finish in ready:
+                finish()
+            if p == 0:
+                made["selected"] = select()
+            if p == 1:
+                made["operators"] = operators(*made["selected"])
             if p < slots:
                 other = k + 1 + p
-                upcoming = paug_ref[other]
-                parts = tapered_by(upcoming, old_high, old_low, pair_index(k - 1, other))
-                upcoming = upcoming + pushed(parts, old_push_high, old_push_low)
-                paug_ref[other] = upcoming
-                if p == 0:
-                    ready.append(upcoming)
-                    ready.append(tapered_by(upcoming, high, low, pair_index(k, other)))
-            if p % 2 == 1:
-                renew_level(p // 2, before, left, mixing)
+                parts = tapered_by(paug_ref[other], old_high, old_low, pair_index(k - 1, other))
+                waiting.append(lambda: finish_slot(p, other, parts))
+            if p in LEVEL_TURNS:
+                level = LEVEL_TURNS.index(p)
+                left, mixing = made["operators"]
+                tapered = crossed_level(level, before, left)
+                waiting.append(lambda: renew_level(level, mixing, tapered))
 
         solved = sweep(covariance, right, root_ref[k], fill)
         push = jnp.where(is_member, -solved, solved)
         push_high, push_low = split(push)
-        paug_ref[k + 1] = ready[0] + pushed(ready[1], push_high, push_low)
+        paug_ref[k + 1] = made["next"] + pushed(made["tapered"], push_high, push_low)
+        for finish in waiting:
+            finish()
         for part, value in enumerate((high, low, push_high, push_low)):
             past_ref[part] = value
         listed_ref[BATCHES] = listed_ref[k]
@@ -439,9 +504,10 @@
             return carry
 
         lax.fori_loop(start, start + SEGMENT, step, 0)
-    left, mixing = operators()
+    left, mixing = operators(*select())
+    tapered = [crossed_level(level, BATCHES - 1, left) for level in range(LEV_DEV)]
     for level in range(LEV_DEV):
-        renew_level(level, BATCHES - 1, left, mixing)
+        renew_level(level, mixing, tapered[level])
     stores = [
         pltpu.make_async_copy(raw_ref.at[c], out_ref.at[:, OBS * c : OBS * c + OBS], sem.at[c])
         for c in range(pieces)

time: 133 us -> 120 us (0.902)
  Pallas kernels: 88.4 us -> 75.9 us
    pallas_call x1, Pallas kernels: 71.8 us -> 59.3 us  [body(): pl.pallas_call(run, name='serial_kernel', out_shape=jax.ShapeDtypeStruct(...]
  transfers between devices with their start and end apart: 4 -> 4, of which waited for: 4 -> 4; matrix products, arithmetic and copies ran while one was open for 0% -> 0% of each run, Pallas kernels for 9% -> 10%
where the time goes in v3:
time: 120 us
  Pallas kernels  75.9 us (63%)
  starting transfers between devices  20.8 us (17%)
  waiting for transfers between devices  16.6 us (14%)
  local copies, waits for them, and re-layouts  3.42 us (3%)
  other arithmetic  2.76 us (2%)
    pallas_call x1, Pallas kernels, body(): pl.pallas_call(run, name='serial_kernel', out_shape=jax.ShapeDtypeStruct(...  59.3 us
    all_to_all x2, starting transfers between devices, sent_to_all(): return lax.all_to_all(copies, axis, split_axis=0, concat_axis=0, tiled=True)  16.6 us
    all_to_all x2, waiting for transfers between devices, sent_to_all(): return lax.all_to_all(copies, axis, split_axis=0, concat_axis=0, tiled=True)  13.3 us
    pallas_call x1, Pallas kernels, body(): pl.pallas_call(index_run, name='index_kernel', out_shape=tuple((jax.Shape...  12.3 us
    pallas_call x1, Pallas kernels, body(): pl.pallas_call(probe_kernel, name='probe_kernel', out_shape=(packed, pack...  4.32 us
  transfers between devices with their start and end apart: 4, of which 4 were waited for; matrix products, arithmetic and copies ran while one was open for 0% of the time, Pallas kernels for 10%

profile of v3, /device:TPU:1, one launch (start us, length us, event | category | flops | bytes accessed | tf_op | source)
XLA Modules:
  0.0 119.6 jit_solution(3504539011892234529)
XLA Ops:
  0.0 0.7 convert_element_type.3
  0.7 0.8 pad_maximum_fusion
  1.5 0.7 broadcast_in_dim.6
  2.1 12.0 %all-to-all-start = ((f32[64,36,2]{1,2,0:T(2,128)}), f32[64,36,2]{1,2,0:T(2,128)S(1)}, u32[]{:S(2)}, u32[]{:S(2)}) async-start(f32[64,36,2]{1,2,0:T(2,128)} %broadcast_in_dim.6), calls=%async_computation | async-start | bytes 131072 | tf_op jit(solution)/shard_map/all_to_all | solution.py:31
  14.1 0.6 pad_add_fusion.place_ref.refs_1_
  14.7 7.8 %all-to-all-done = f32[64,36,2]{1,2,0:T(2,128)S(1)} async-done(((f32[64,36,2]{1,2,0:T(2,128)}), f32[64,36,2]{1,2,0:T(2,128)S(1)}, u32[]{:S(2)}, u32[]{:S(2)}) %all-to-all-start) | async-done | bytes 18464 | tf_op jit(solution)/shard_map/all_to_all | solution.py:31
  22.5 0.7 copy.9.table_ref.refs_3_
  23.2 4.3 %probe_kernel.1 = (f32[32,128]{1,0:T(8,128)}, f32[32,128]{1,0:T(8,128)}) custom-call(s32[2]{0:T(128)} %pad_add_fusion.place_ref.refs_1_, f32[640,1024]{1,0:T(8,128)} %bitcast.10, f32[36,128]{1,0:T(8,128)} %copy.9.table_ref.refs_3_, f32[12,8,128]{2,1,0:T(8,128)} %weight_ref.1), custom_call_target="tpu_custom_call" | custom-call | tf_op jit(solution)/shard_map/probe_kernel/pallas_call | solution.py:535
  27.5 2.2 %collective-permute-start = (f32[32,128]{1,0:T(8,128)}, f32[32,128]{1,0:T(8,128)S(1)}, u32[]{:S(2)}, u32[]{:S(2)}) collective-permute-start(f32[32,128]{1,0:T(8,128)} %get-tuple-element.20), channel_id=1, source_target_pairs={{0,1},{1,0},{2,3},{3,2},{4,5},{5,4},{6,7},{7,6},{8,9},{9,8},{10,11... | collective-permute-start | bytes 49160 | tf_op jit(solution)/shard_map/ppermute | solution.py:549
  29.7 1.0 collective-permute-done
  30.7 0.7 add.11.refs_2_
  31.5 0.0 copy-start.2
  31.5 1.1 broadcast_in_dim.7
  32.6 4.7 %all-to-all-start.1 = ((f32[64,32,128]{2,1,0:T(8,128)}), f32[64,32,128]{2,1,0:T(8,128)S(1)}, u32[]{:S(2)}, u32[]{:S(2)}) async-start(f32[64,32,128]{2,1,0:T(8,128)} %broadcast_in_dim.7), calls=%async_computation.1 | async-start | bytes 2097152 | tf_op jit(solution)/shard_map/all_to_all | solution.py:31
  37.3 0.0 copy-done.2
  37.3 12.3 %index_kernel.1 = (f32[8,80,1024]{2,1,0:T(8,128)}, f32[66,128,128]{2,1,0:T(8,128)}, f32[12,32,1024]{2,1,0:T(8,128)}, f32[13,32,128]{2,1,0:T(8,128)}, f32[12,128,...) custom-call(s32[12]{0:T(128)} %refs_0_.3, ...), custom_call_target="tpu_custom_call" | custom-call | flops 41943040 | bytes 16777216 | tf_op jit(solution)/shard_map/index_kernel/pallas_call | solution.py:577
  49.5 5.5 %all-to-all-done.1 = f32[64,32,128]{2,1,0:T(8,128)S(1)} async-done(((f32[64,32,128]{2,1,0:T(8,128)}), f32[64,32,128]{2,1,0:T(8,128)S(1)}, u32[]{:S(2)}, u32[]{:S(2)}) %all-to-all-start.1) | async-done | bytes 1048608 | tf_op jit(solution)/shard_map/all_to_all | solution.py:31
  55.0 0.0 copy-start
  55.0 1.9 %collective-permute-start.1 = (f32[64,32,128]{2,1,0:T(8,128)S(1)}, f32[64,32,128]{2,1,0:T(8,128)S(1)}, u32[]{:S(2)}, u32[]{:S(2)}) collective-permute-start(f32[64,32,128]{2,1,0:T(8,128)S(1)} %all-to-all-done.1), channel_id=1, source_target_pairs={{0,1},{1,0},{2,3},{3,2},{4,5},{5,4},{6,7},{7,6},{8,9},{9,8},{10,11... | collective-permute-start | bytes 3145736 | tf_op jit(solution)/shard_map/ppermute | solution.py:599
  56.9 2.3 %collective-permute-done.1 = f32[64,32,128]{2,1,0:T(8,128)S(1)} collective-permute-done((f32[64,32,128]{2,1,0:T(8,128)S(1)}, f32[64,32,128]{2,1,0:T(8,128)S(1)}, u32[]{:S(2)}, u32[]{:S(2)}) %collective-permute-start.1) | collective-permute-done | bytes 1048608 | tf_op jit(solution)/shard_map/ppermute | solution.py:599
  59.2 0.0 copy-start.1
  59.2 0.0 copy-done
  59.2 1.0 copy-done.1
  60.2 59.3 %serial_kernel.1 = f32[640,1024]{1,0:T(8,128)} custom-call(s32[12]{0:T(128)} %refs_0_.3, s32[2]{0:T(128)} %pad_add_fusion.place_ref.refs_1_, f32[2048,128]{1,0:T(8,128)} %bitcast.9, f32[2048,128]{1,0:T(8,128)} %bitcast.12, f32[8,128]{1,0:T(8,128)} %get-tuple-element.23.refs_4_, f32[8,80,1024]{2,1,0:T(8,128)} %get-tuple-element.24.refs_5_, ...), custom_call_target="tpu_custom_call" | custom-call | tf_op jit(solution)/shard_map/serial_kernel/pallas_call | solution.py:606
Async XLA Ops:
  2.1 20.4 %all-to-all-start = ((f32[64,36,2]{1,2,0:T(2,128)}), f32[64,36,2]{1,2,0:T(2,128)S(1)}, u32[]{:S(2)}, u32[]{:S(2)}) async-start(f32[64,36,2]{1,2,0:T(2,128)} %broadcast_in_dim.6), calls=%async_computation | async-start | bytes 131072 | tf_op jit(solution)/shard_map/all_to_all | solution.py:31
  27.5 3.2 %collective-permute-start = (f32[32,128]{1,0:T(8,128)}, f32[32,128]{1,0:T(8,128)S(1)}, u32[]{:S(2)}, u32[]{:S(2)}) collective-permute-start(f32[32,128]{1,0:T(8,128)} %get-tuple-element.20), channel_id=1, source_target_pairs={{0,1},{1,0},{2,3},{3,2},{4,5},{5,4},{6,7},{7,6},{8,9},{9,8},{10,11... | collective-permute-start | bytes 49160 | tf_op jit(solution)/shard_map/ppermute | solution.py:549
  31.5 5.8 %copy-start.2 = (f32[32,128]{1,0:T(8,128)}, f32[32,128]{1,0:T(8,128)S(1)}, u32[]{:S(2)}) copy-start(f32[32,128]{1,0:T(8,128)S(1)} %add.11.refs_2_) | copy-start | bytes 49156
  32.6 22.4 %all-to-all-start.1 = ((f32[64,32,128]{2,1,0:T(8,128)}), f32[64,32,128]{2,1,0:T(8,128)S(1)}, u32[]{:S(2)}, u32[]{:S(2)}) async-start(f32[64,32,128]{2,1,0:T(8,128)} %broadcast_in_dim.7), calls=%async_computation.1 | async-start | bytes 2097152 | tf_op jit(solution)/shard_map/all_to_all | solution.py:31
  55.0 4.2 %copy-start = (f32[64,32,128]{2,1,0:T(8,128)}, f32[64,32,128]{2,1,0:T(8,128)S(1)}, u32[]{:S(2)}) copy-start(f32[64,32,128]{2,1,0:T(8,128)S(1)} %all-to-all-done.1) | copy-start | bytes 3145732
  55.0 4.2 %collective-permute-start.1 = (f32[64,32,128]{2,1,0:T(8,128)S(1)}, f32[64,32,128]{2,1,0:T(8,128)S(1)}, u32[]{:S(2)}, u32[]{:S(2)}) collective-permute-start(f32[64,32,128]{2,1,0:T(8,128)S(1)} %all-to-all-done.1), channel_id=1, source_target_pairs={{0,1},{1,0},{2,3},{3,2},{4,5},{5,4},{6,7},{7,6},{8,9},{9,8},{10,11... | collective-permute-start | bytes 3145736 | tf_op jit(solution)/shard_map/ppermute | solution.py:599
  59.2 1.0 copy-start.1

commit v4 on v3

--- a/solution.py
+++ b/solution.py
@@ -19,6 +19,7 @@
 PACK = 32
 SEGMENT = 4
 LAG = 3
+CHUNKS = 4
 WIDE = 16
 LEVEL_TURNS = (2, 4, 6, 8, 10, 11, 12, 13)
 LON = ("lon_0", "lon_1", "lon_2")
@@ -58,8 +59,13 @@
 
 def probe_kernel(place_ref, ens_ref, table_ref, weight_ref, keep_ref, send_ref, turn_ref, block_ref, sem):
     tile, level_half = place_ref[0], place_ref[1]
-    fetch = pltpu.make_async_copy(ens_ref, block_ref, sem)
-    fetch.start()
+    width = CELL_DEV // CHUNKS
+    fetches = [
+        pltpu.make_async_copy(ens_ref.at[:, width * c : width * c + width], block_ref.at[c], sem.at[c])
+        for c in range(CHUNKS)
+    ]
+    for fetch in fetches:
+        fetch.start()
     cells = table_ref[0:16, :].astype(jnp.int32)
     own = (cells >> 10) == tile
     lane = iota((OBS, OBS), 1)
@@ -91,11 +97,13 @@
         picked = picked + dot(left, chosen)
     cell = picked[0:1, :] * LON_DEV + picked[1:2, :]
     weight = picked[8:16, :] + picked[16:24, :] + picked[24:32, :]
-    column = iota((CELL_DEV, OBS), 0).astype(f32)
-    one_hot = (column == cell).astype(f32).astype(bf16)
-    fetch.wait()
-    high, low = split(block_ref[...])
-    taken = dot(high, one_hot) + dot(low, one_hot)
+    column = iota((width, OBS), 0).astype(f32)
+    taken = jnp.zeros((MEM * LEV_DEV, OBS), f32)
+    for c in range(CHUNKS):
+        one_hot = (column + float(width * c) == cell).astype(f32).astype(bf16)
+        fetches[c].wait()
+        high, low = split(block_ref[c])
+        taken = taken + (dot(high, one_hot) + dot(low, one_hot))
     summed = jnp.sum(taken.reshape(MEM, LEV_DEV, OBS) * weight[None], axis=1)
     turn_ref[...] = jnp.zeros((OBS, OBS), f32)
     turn_ref[0:MEM, :] = summed
@@ -135,6 +143,12 @@
     high, mid, low = (placed(part) for part in split3(rows))
     right = jnp.concatenate([high, high, high, mid, mid, low], axis=0)
     return dot(factors, right)
+
+
+def added(terms):
+    while len(terms) > 1:
+        terms = [x + y for x, y in zip(terms[::2], terms[1::2])]
+    return terms[0]
 
 
 def sweep(covariance, right, root, fill):
@@ -159,7 +173,13 @@
             block, at = divmod(j, 8)
             at_j = sub == at
             pivot = sub_of(columns[j][block], at)
-            inverse = 1.0 / pivot
+            if j % 2 == 0:
+                inverse = 1.0 / pivot
+                beside = sub_of(columns[j + 1][block], at)
+                corner = sub_of(columns[j + 1][block], at + 1)
+                inverse_next = pivot / (pivot * corner - beside * beside)
+            else:
+                inverse = inverse_next
             others = list(columns[j])
             others[block] = jnp.where(at_j, 0.0, others[block])
             factor = [other * inverse for other in others]
@@ -179,11 +199,9 @@
         a = [x * s for x, s in zip(a, scale)]
         b = [x * s for x, s in zip(b, scale)]
         for i in near:
-            old = left_rows[i]
-            for r in range(WIDE):
-                factor = lane_of(old, base + r)
-                left_rows[i] = left_rows[i] - factor * sub_of(a[r // 8], r % 8)
-                right_rows[i] = right_rows[i] - factor * sub_of(b[r // 8], r % 8)
+            factor = [lane_of(left_rows[i], base + r) for r in range(WIDE)]
+            left_rows[i] = left_rows[i] - added([factor[r] * sub_of(a[r // 8], r % 8) for r in range(WIDE)])
+            right_rows[i] = right_rows[i] - added([factor[r] * sub_of(b[r // 8], r % 8) for r in range(WIDE)])
         far = [i for i in range(blocks) if i not in own and i not in near]
         change = product_of_panel(factors, jnp.concatenate(b, axis=0), panel)
         for i in far:
@@ -347,6 +365,7 @@
     raw_ref,
     paug_ref,
     past_ref,
+    soon_ref,
     sem,
     sent_sem,
 ):
@@ -361,12 +380,13 @@
         (pair_sent, pair_ref),
         (state_sent, state_ref),
     )
+    first_pair = pltpu.make_async_copy(pair_sent.at[0:1], soon_ref, sem.at[0])
+    first_pair.start()
     fetches = [pltpu.make_async_copy(a, b, sent_sem.at[n]) for n, (a, b) in enumerate(moves)]
     for fetch in fetches:
         fetch.start()
     for fetch in fetches[:2]:
         fetch.wait()
-    pieces = CELL_DEV // OBS
     square = (OBS, OBS)
     lane = iota(square, 1)
     lane_f = lane.astype(f32)
@@ -399,8 +419,9 @@
         mean = jnp.sum(gathered, axis=1, keepdims=True) * (1.0 / MEM)
         mean = jnp.broadcast_to(mean, square)
         paug_ref[k] = jnp.where(is_member, gathered - mean, jnp.where(lane == MEM, mean, 0.0))
-    for fetch in fetches[2:]:
+    for fetch in fetches[2:6]:
         fetch.wait()
+    first_pair.wait()
 
     is_member_s = is_member[0:ROWS]
     lane_s = lane[0:ROWS]
@@ -425,21 +446,25 @@
         stacked = jnp.concatenate([gain_high, gain_high, gain - gain_high, jnp.zeros_like(gain)], axis=0)
         return left, stacked.T[0:MEM, :].astype(bf16)
 
-    def crossed_level(level, before, left):
-        x_high, x_low = split(state_ref[level])
-        filler = jnp.zeros((16, CELL_DEV), bf16)
+    def crossed_level(level, before, left, part=slice(0, CELL_DEV)):
+        width = part.stop - part.start
+        x_high, x_low = split(state_ref[level, :, part])
+        filler = jnp.zeros((16, width), bf16)
         crossed = dot(left, jnp.concatenate([x_high, x_low, x_high, filler], axis=0))
-        t_high, t_low = split(crossed * local_ref[before])
-        filler = jnp.zeros((ROWS, CELL_DEV), bf16)
+        t_high, t_low = split(crossed * local_ref[before, :, part])
+        filler = jnp.zeros((ROWS, width), bf16)
         return jnp.concatenate([t_high, t_low, t_high, filler], axis=0)
 
     def renew_level(level, mixing, tapered):
         state_ref[level] = state_ref[level] + dot(mixing, tapered)
 
-    def tapered_by(upcoming, high, low, pair):
+    def pair_weight(pair):
+        return pair_ref[jnp.clip(pair, 0, last_pair)]
+
+    def tapered_by(upcoming, high, low, weight):
         up_high, up_low = split(jnp.where(is_member, upcoming, 0.0))
         crossed = dot_lanes(up_high, high) + dot_lanes(up_low, high) + dot_lanes(up_high, low)
-        return split(crossed * pair_ref[jnp.clip(pair, 0, last_pair)])
+        return split(crossed * weight)
 
     def pushed(parts, push_high, push_low):
         t_high, t_low = parts
@@ -462,13 +487,18 @@
                 made["next"] = upcoming
 
                 def taper_next():
-                    made["tapered"] = tapered_by(upcoming, high, low, pair_index(k, other))
+                    made["tapered"] = tapered_by(upcoming, high, low, pair_weight(pair_index(k, other)))
 
                 waiting.append(taper_next)
             else:
                 paug_ref[other] = upcoming
 
         def fill(p):
+            if slots is None:
+                if p == 0:
+                    made["next"] = paug_ref[1]
+                    made["tapered"] = tapered_by(made["next"], high, low, soon_ref[0])
+                return
             ready = waiting[:-LAG] if p < OBS // 8 - 1 else waiting[:]
             del waiting[: len(ready)]
             for finish in ready:
@@ -479,7 +509,7 @@
                 made["operators"] = operators(*made["selected"])
             if p < slots:
                 other = k + 1 + p
-                parts = tapered_by(paug_ref[other], old_high, old_low, pair_index(k - 1, other))
+                parts = tapered_by(paug_ref[other], old_high, old_low, pair_weight(pair_index(k - 1, other)))
                 waiting.append(lambda: finish_slot(p, other, parts))
             if p in LEVEL_TURNS:
                 level = LEVEL_TURNS.index(p)
@@ -497,25 +527,33 @@
             past_ref[part] = value
         listed_ref[BATCHES] = listed_ref[k]
 
+    turn(0, None)
+    for fetch in fetches[6:]:
+        fetch.wait()
     for start in range(0, BATCHES, SEGMENT):
+        begin = max(start, 1)
 
         def step(k, carry):
-            turn(k, BATCHES - 1 - start)
+            turn(k, BATCHES - 1 - begin)
             return carry
 
-        lax.fori_loop(start, start + SEGMENT, step, 0)
+        lax.fori_loop(begin, start + SEGMENT, step, 0)
     left, mixing = operators(*select())
-    tapered = [crossed_level(level, BATCHES - 1, left) for level in range(LEV_DEV)]
-    for level in range(LEV_DEV):
-        renew_level(level, mixing, tapered[level])
+    pieces = CELL_DEV // OBS
     stores = [
         pltpu.make_async_copy(raw_ref.at[c], out_ref.at[:, OBS * c : OBS * c + OBS], sem.at[c])
         for c in range(pieces)
     ]
-    for c in range(pieces):
+    for c in range(0, pieces, 2):
+        part = slice(OBS * c, OBS * c + 2 * OBS)
+        tapered = [crossed_level(level, BATCHES - 1, left, part) for level in range(LEV_DEV)]
         for level in range(LEV_DEV):
-            raw_ref[c, pl.ds(level, MEM, stride=LEV_DEV), :] = state_ref[level, :, OBS * c : OBS * c + OBS]
+            block = state_ref[level, :, part] + dot(mixing, tapered[level])
+            rows = pl.ds(level, MEM, stride=LEV_DEV)
+            raw_ref[c, rows, :] = block[:, 0:OBS]
+            raw_ref[c + 1, rows, :] = block[:, OBS : 2 * OBS]
         stores[c].start()
+        stores[c + 1].start()
     for store in stores:
         store.wait()
 
@@ -540,8 +578,8 @@
         out_specs=(whole(pltpu.VMEM), whole(pltpu.VMEM)),
         scratch_shapes=[
             pltpu.VMEM((OBS, OBS), f32),
-            pltpu.VMEM(flat.shape, f32),
-            pltpu.SemaphoreType.DMA,
+            pltpu.VMEM((CHUNKS, MEM * LEV_DEV, CELL_DEV // CHUNKS), f32),
+            pltpu.SemaphoreType.DMA((CHUNKS,)),
         ],
         compiler_params=pltpu.CompilerParams(vmem_limit_bytes=62 << 20),
     )(place, flat, table, obs_weight)
@@ -616,6 +654,7 @@
             pltpu.VMEM(raw_shape, f32),
             pltpu.VMEM((2 * BATCHES, OBS, OBS), f32),
             pltpu.VMEM((4, OBS, OBS), bf16),
+            pltpu.VMEM((1, OBS, OBS), f32),
             pltpu.SemaphoreType.DMA((CELL_DEV // OBS,)),
             pltpu.SemaphoreType.DMA((len(shapes) - 1,)),
         ],

time: 120 us -> 119 us (level)
  Pallas kernels: 75.9 us -> 74.4 us
    pallas_call x1, Pallas kernels: 59.3 us -> 57.7 us  [body(): pl.pallas_call(run, name='serial_kernel', out_shape=jax.ShapeDtypeStruct(...]
where the time goes in v4:
time: 119 us; the launch traced here: 118 us
  Pallas kernels  74.4 us (63%)
  starting transfers between devices  20.8 us (17%)
  waiting for transfers between devices  16.6 us (14%)
  local copies, waits for them, and re-layouts  3.42 us (3%)
  other arithmetic  2.76 us (2%)
    pallas_call x1, Pallas kernels, body(): pl.pallas_call(run, name='serial_kernel', out_shape=jax.ShapeDtypeStruct(...  57.7 us
    all_to_all x2, starting transfers between devices, sent_to_all(): return lax.all_to_all(copies, axis, split_axis=0, concat_axis=0, tiled=True)  16.7 us
    all_to_all x2, waiting for transfers between devices, sent_to_all(): return lax.all_to_all(copies, axis, split_axis=0, concat_axis=0, tiled=True)  13.3 us
    pallas_call x1, Pallas kernels, body(): pl.pallas_call(index_run, name='index_kernel', out_shape=tuple((jax.Shape...  12.3 us
    pallas_call x1, Pallas kernels, body(): pl.pallas_call(probe_kernel, name='probe_kernel', out_shape=(packed, pack...  4.37 us
  transfers between devices with their start and end apart: 4, of which 4 were waited for; matrix products, arithmetic and copies ran while one was open for 0% of the time, Pallas kernels for 10%

profile of v4, /device:TPU:1, one launch (start us, length us, event | category | flops | bytes accessed | tf_op | source)
XLA Modules:
  0.0 118.2 jit_solution(3001420144358524296)
XLA Ops:
  0.0 0.7 convert_element_type.3
  0.7 0.8 pad_maximum_fusion
  1.5 0.7 broadcast_in_dim.6
  2.1 12.0 %all-to-all-start = ((f32[64,36,2]{1,2,0:T(2,128)}), f32[64,36,2]{1,2,0:T(2,128)S(1)}, u32[]{:S(2)}, u32[]{:S(2)}) async-start(f32[64,36,2]{1,2,0:T(2,128)} %broadcast_in_dim.6), calls=%async_computation | async-start | bytes 131072 | tf_op jit(solution)/shard_map/all_to_all | solution.py:32
  14.1 0.6 pad_add_fusion.place_ref.refs_1_
  14.7 7.8 %all-to-all-done = f32[64,36,2]{1,2,0:T(2,128)S(1)} async-done(((f32[64,36,2]{1,2,0:T(2,128)}), f32[64,36,2]{1,2,0:T(2,128)S(1)}, u32[]{:S(2)}, u32[]{:S(2)}) %all-to-all-start) | async-done | bytes 18464 | tf_op jit(solution)/shard_map/all_to_all | solution.py:32
  22.5 0.7 copy.9.table_ref.refs_3_
  23.2 4.4 %probe_kernel.1 = (f32[32,128]{1,0:T(8,128)}, f32[32,128]{1,0:T(8,128)}) custom-call(s32[2]{0:T(128)} %pad_add_fusion.place_ref.refs_1_, f32[640,1024]{1,0:T(8,128)} %bitcast.10, f32[36,128]{1,0:T(8,128)} %copy.9.table_ref.refs_3_, f32[12,8,128]{2,1,0:T(8,128)} %weight_ref.1), custom_call_target="tpu_custom_call" | custom-call | tf_op jit(solution)/shard_map/probe_kernel/pallas_call | solution.py:573
  27.6 2.2 %collective-permute-start = (f32[32,128]{1,0:T(8,128)}, f32[32,128]{1,0:T(8,128)S(1)}, u32[]{:S(2)}, u32[]{:S(2)}) collective-permute-start(f32[32,128]{1,0:T(8,128)} %get-tuple-element.20), channel_id=1, source_target_pairs={{0,1},{1,0},{2,3},{3,2},{4,5},{5,4},{6,7},{7,6},{8,9},{9,8},{10,11... | collective-permute-start | bytes 49160 | tf_op jit(solution)/shard_map/ppermute | solution.py:587
  29.7 1.0 collective-permute-done
  30.8 0.7 add.11.refs_2_
  31.5 0.0 copy-start.2
  31.5 1.1 broadcast_in_dim.7
  32.6 4.7 %all-to-all-start.1 = ((f32[64,32,128]{2,1,0:T(8,128)}), f32[64,32,128]{2,1,0:T(8,128)S(1)}, u32[]{:S(2)}, u32[]{:S(2)}) async-start(f32[64,32,128]{2,1,0:T(8,128)} %broadcast_in_dim.7), calls=%async_computation.1 | async-start | bytes 2097152 | tf_op jit(solution)/shard_map/all_to_all | solution.py:32
  37.3 0.0 copy-done.2
  37.3 12.3 %index_kernel.1 = (f32[8,80,1024]{2,1,0:T(8,128)}, f32[66,128,128]{2,1,0:T(8,128)}, f32[12,32,1024]{2,1,0:T(8,128)}, f32[13,32,128]{2,1,0:T(8,128)}, f32[12,128,...) custom-call(s32[12]{0:T(128)} %refs_0_.3, ...), custom_call_target="tpu_custom_call" | custom-call | flops 41943040 | bytes 16777216 | tf_op jit(solution)/shard_map/index_kernel/pallas_call | solution.py:615
  49.6 5.5 %all-to-all-done.1 = f32[64,32,128]{2,1,0:T(8,128)S(1)} async-done(((f32[64,32,128]{2,1,0:T(8,128)}), f32[64,32,128]{2,1,0:T(8,128)S(1)}, u32[]{:S(2)}, u32[]{:S(2)}) %all-to-all-start.1) | async-done | bytes 1048608 | tf_op jit(solution)/shard_map/all_to_all | solution.py:32
  55.0 0.0 copy-start
  55.0 1.9 %collective-permute-start.1 = (f32[64,32,128]{2,1,0:T(8,128)S(1)}, f32[64,32,128]{2,1,0:T(8,128)S(1)}, u32[]{:S(2)}, u32[]{:S(2)}) collective-permute-start(f32[64,32,128]{2,1,0:T(8,128)S(1)} %all-to-all-done.1), channel_id=1, source_target_pairs={{0,1},{1,0},{2,3},{3,2},{4,5},{5,4},{6,7},{7,6},{8,9},{9,8},{10,11... | collective-permute-start | bytes 3145736 | tf_op jit(solution)/shard_map/ppermute | solution.py:637
  57.0 2.3 %collective-permute-done.1 = f32[64,32,128]{2,1,0:T(8,128)S(1)} collective-permute-done((f32[64,32,128]{2,1,0:T(8,128)S(1)}, f32[64,32,128]{2,1,0:T(8,128)S(1)}, u32[]{:S(2)}, u32[]{:S(2)}) %collective-permute-start.1) | collective-permute-done | bytes 1048608 | tf_op jit(solution)/shard_map/ppermute | solution.py:637
  59.3 0.0 copy-start.1
  59.3 0.0 copy-done
  59.3 1.0 copy-done.1
  60.3 57.7 %serial_kernel.1 = f32[640,1024]{1,0:T(8,128)} custom-call(s32[12]{0:T(128)} %refs_0_.3, s32[2]{0:T(128)} %pad_add_fusion.place_ref.refs_1_, f32[2048,128]{1,0:T(8,128)} %bitcast.9, f32[2048,128]{1,0:T(8,128)} %bitcast.12, f32[8,128]{1,0:T(8,128)} %get-tuple-element.23.refs_4_, f32[8,80,1024]{2,1,0:T(8,128)} %get-tuple-element.24.refs_5_, ...), custom_call_target="tpu_custom_call" | custom-call | tf_op jit(solution)/shard_map/serial_kernel/pallas_call | solution.py:644
Async XLA Ops:
  2.1 20.4 %all-to-all-start = ((f32[64,36,2]{1,2,0:T(2,128)}), f32[64,36,2]{1,2,0:T(2,128)S(1)}, u32[]{:S(2)}, u32[]{:S(2)}) async-start(f32[64,36,2]{1,2,0:T(2,128)} %broadcast_in_dim.6), calls=%async_computation | async-start | bytes 131072 | tf_op jit(solution)/shard_map/all_to_all | solution.py:32
  27.6 3.2 %collective-permute-start = (f32[32,128]{1,0:T(8,128)}, f32[32,128]{1,0:T(8,128)S(1)}, u32[]{:S(2)}, u32[]{:S(2)}) collective-permute-start(f32[32,128]{1,0:T(8,128)} %get-tuple-element.20), channel_id=1, source_target_pairs={{0,1},{1,0},{2,3},{3,2},{4,5},{5,4},{6,7},{7,6},{8,9},{9,8},{10,11... | collective-permute-start | bytes 49160 | tf_op jit(solution)/shard_map/ppermute | solution.py:587
  31.5 5.8 %copy-start.2 = (f32[32,128]{1,0:T(8,128)}, f32[32,128]{1,0:T(8,128)S(1)}, u32[]{:S(2)}) copy-start(f32[32,128]{1,0:T(8,128)S(1)} %add.11.refs_2_) | copy-start | bytes 49156
  32.6 22.4 %all-to-all-start.1 = ((f32[64,32,128]{2,1,0:T(8,128)}), f32[64,32,128]{2,1,0:T(8,128)S(1)}, u32[]{:S(2)}, u32[]{:S(2)}) async-start(f32[64,32,128]{2,1,0:T(8,128)} %broadcast_in_dim.7), calls=%async_computation.1 | async-start | bytes 2097152 | tf_op jit(solution)/shard_map/all_to_all | solution.py:32
  55.0 4.2 %copy-start = (f32[64,32,128]{2,1,0:T(8,128)}, f32[64,32,128]{2,1,0:T(8,128)S(1)}, u32[]{:S(2)}) copy-start(f32[64,32,128]{2,1,0:T(8,128)S(1)} %all-to-all-done.1) | copy-start | bytes 3145732
  55.0 4.2 %collective-permute-start.1 = (f32[64,32,128]{2,1,0:T(8,128)S(1)}, f32[64,32,128]{2,1,0:T(8,128)S(1)}, u32[]{:S(2)}, u32[]{:S(2)}) collective-permute-start(f32[64,32,128]{2,1,0:T(8,128)S(1)} %all-to-all-done.1), channel_id=1, source_target_pairs={{0,1},{1,0},{2,3},{3,2},{4,5},{5,4},{6,7},{7,6},{8,9},{9,8},{10,11... | collective-permute-start | bytes 3145736 | tf_op jit(solution)/shard_map/ppermute | solution.py:637
  59.3 1.0 copy-start.1

commit v5 on v4

--- a/solution.py
+++ b/solution.py
@@ -222,8 +222,8 @@
     rest = spread - high.astype(f32)
     mid = rest.astype(bf16)
     low = (rest - mid.astype(f32)).astype(bf16)
-    small = dot_lanes(high, low) + dot_lanes(low, high) + dot_lanes(mid, mid)
-    return dot_lanes(high, high) + (dot_lanes(high, mid) + dot_lanes(mid, high) + small)
+    left = jnp.concatenate([high, high, mid, high, low, mid], axis=1)
+    return dot_lanes(left, jnp.concatenate([high, mid, high, low, high, mid], axis=1))
 
 
 def taper(rows_a, cols_a, rows_b, cols_b, circle):
@@ -463,12 +463,14 @@
 
     def tapered_by(upcoming, high, low, weight):
         up_high, up_low = split(jnp.where(is_member, upcoming, 0.0))
-        crossed = dot_lanes(up_high, high) + dot_lanes(up_low, high) + dot_lanes(up_high, low)
+        left = jnp.concatenate([up_high, up_low, up_high], axis=1)
+        crossed = dot_lanes(left, jnp.concatenate([high, high, low], axis=1))
         return split(crossed * weight)
 
     def pushed(parts, push_high, push_low):
         t_high, t_low = parts
-        return dot(t_high, push_high) + dot(t_low, push_high) + dot(t_high, push_low)
+        left = jnp.concatenate([t_high, t_low, t_high], axis=1)
+        return dot(left, jnp.concatenate([push_high, push_high, push_low], axis=0))
 
     def turn(k, slots):
         before = jnp.maximum(k - 1, 0)

time: 119 us -> 118 us (level)
  no operation moved by 1% of the time
where the time goes in v5:
time: 118 us
  Pallas kernels  73.9 us (63%)
  starting transfers between devices  20.8 us (18%)
  waiting for transfers between devices  16.6 us (14%)
  local copies, waits for them, and re-layouts  3.42 us (3%)
  other arithmetic  2.76 us (2%)
    pallas_call x1, Pallas kernels, body(): pl.pallas_call(run, name='serial_kernel', out_shape=jax.ShapeDtypeStruct(...  57.3 us
    all_to_all x2, starting transfers between devices, sent_to_all(): return lax.all_to_all(copies, axis, split_axis=0, concat_axis=0, tiled=True)  16.7 us
    all_to_all x2, waiting for transfers between devices, sent_to_all(): return lax.all_to_all(copies, axis, split_axis=0, concat_axis=0, tiled=True)  13.3 us
    pallas_call x1, Pallas kernels, body(): pl.pallas_call(index_run, name='index_kernel', out_shape=tuple((jax.Shape...  12.3 us
    pallas_call x1, Pallas kernels, body(): pl.pallas_call(probe_kernel, name='probe_kernel', out_shape=(packed, pack...  4.37 us
  transfers between devices with their start and end apart: 4, of which 4 were waited for; matrix products, arithmetic and copies ran while one was open for 0% of the time, Pallas kernels for 10%

profile of v5, /device:TPU:1, one launch (start us, length us, event | category | flops | bytes accessed | tf_op | source)
XLA Modules:
  0.0 117.7 jit_solution(7965419159915969378)
XLA Ops:
  0.0 0.7 convert_element_type.3
  0.7 0.8 pad_maximum_fusion
  1.5 0.7 broadcast_in_dim.6
  2.1 12.0 %all-to-all-start = ((f32[64,36,2]{1,2,0:T(2,128)}), f32[64,36,2]{1,2,0:T(2,128)S(1)}, u32[]{:S(2)}, u32[]{:S(2)}) async-start(f32[64,36,2]{1,2,0:T(2,128)} %broadcast_in_dim.6), calls=%async_computation | async-start | bytes 131072 | tf_op jit(solution)/shard_map/all_to_all | solution.py:32
  14.1 0.6 pad_add_fusion.place_ref.refs_1_
  14.7 7.8 %all-to-all-done = f32[64,36,2]{1,2,0:T(2,128)S(1)} async-done(((f32[64,36,2]{1,2,0:T(2,128)}), f32[64,36,2]{1,2,0:T(2,128)S(1)}, u32[]{:S(2)}, u32[]{:S(2)}) %all-to-all-start) | async-done | bytes 18464 | tf_op jit(solution)/shard_map/all_to_all | solution.py:32
  22.5 0.7 copy.9.table_ref.refs_3_
  23.2 4.4 %probe_kernel.1 = (f32[32,128]{1,0:T(8,128)}, f32[32,128]{1,0:T(8,128)}) custom-call(s32[2]{0:T(128)} %pad_add_fusion.place_ref.refs_1_, f32[640,1024]{1,0:T(8,128)} %bitcast.10, f32[36,128]{1,0:T(8,128)} %copy.9.table_ref.refs_3_, f32[12,8,128]{2,1,0:T(8,128)} %weight_ref.1), custom_call_target="tpu_custom_call" | custom-call | tf_op jit(solution)/shard_map/probe_kernel/pallas_call | solution.py:575
  27.6 2.2 %collective-permute-start = (f32[32,128]{1,0:T(8,128)}, f32[32,128]{1,0:T(8,128)S(1)}, u32[]{:S(2)}, u32[]{:S(2)}) collective-permute-start(f32[32,128]{1,0:T(8,128)} %get-tuple-element.20), channel_id=1, source_target_pairs={{0,1},{1,0},{2,3},{3,2},{4,5},{5,4},{6,7},{7,6},{8,9},{9,8},{10,11... | collective-permute-start | bytes 49160 | tf_op jit(solution)/shard_map/ppermute | solution.py:589
  29.7 1.0 collective-permute-done
  30.8 0.7 add.11.refs_2_
  31.5 0.0 copy-start.2
  31.5 1.1 broadcast_in_dim.7
  32.6 4.7 %all-to-all-start.1 = ((f32[64,32,128]{2,1,0:T(8,128)}), f32[64,32,128]{2,1,0:T(8,128)S(1)}, u32[]{:S(2)}, u32[]{:S(2)}) async-start(f32[64,32,128]{2,1,0:T(8,128)} %broadcast_in_dim.7), calls=%async_computation.1 | async-start | bytes 2097152 | tf_op jit(solution)/shard_map/all_to_all | solution.py:32
  37.3 0.0 copy-done.2
  37.3 12.3 %index_kernel.1 = (f32[8,80,1024]{2,1,0:T(8,128)}, f32[66,128,128]{2,1,0:T(8,128)}, f32[12,32,1024]{2,1,0:T(8,128)}, f32[13,32,128]{2,1,0:T(8,128)}, f32[12,128,...) custom-call(s32[12]{0:T(128)} %refs_0_.3, ...), custom_call_target="tpu_custom_call" | custom-call | flops 41943040 | bytes 16777216 | tf_op jit(solution)/shard_map/index_kernel/pallas_call | solution.py:617
  49.6 5.4 %all-to-all-done.1 = f32[64,32,128]{2,1,0:T(8,128)S(1)} async-done(((f32[64,32,128]{2,1,0:T(8,128)}), f32[64,32,128]{2,1,0:T(8,128)S(1)}, u32[]{:S(2)}, u32[]{:S(2)}) %all-to-all-start.1) | async-done | bytes 1048608 | tf_op jit(solution)/shard_map/all_to_all | solution.py:32
  55.0 0.0 copy-start
  55.0 1.9 %collective-permute-start.1 = (f32[64,32,128]{2,1,0:T(8,128)S(1)}, f32[64,32,128]{2,1,0:T(8,128)S(1)}, u32[]{:S(2)}, u32[]{:S(2)}) collective-permute-start(f32[64,32,128]{2,1,0:T(8,128)S(1)} %all-to-all-done.1), channel_id=1, source_target_pairs={{0,1},{1,0},{2,3},{3,2},{4,5},{5,4},{6,7},{7,6},{8,9},{9,8},{10,11... | collective-permute-start | bytes 3145736 | tf_op jit(solution)/shard_map/ppermute | solution.py:639
  57.0 2.3 %collective-permute-done.1 = f32[64,32,128]{2,1,0:T(8,128)S(1)} collective-permute-done((f32[64,32,128]{2,1,0:T(8,128)S(1)}, f32[64,32,128]{2,1,0:T(8,128)S(1)}, u32[]{:S(2)}, u32[]{:S(2)}) %collective-permute-start.1) | collective-permute-done | bytes 1048608 | tf_op jit(solution)/shard_map/ppermute | solution.py:639
  59.3 0.0 copy-start.1
  59.3 0.0 copy-done
  59.3 1.0 copy-done.1
  60.3 57.3 %serial_kernel.1 = f32[640,1024]{1,0:T(8,128)} custom-call(s32[12]{0:T(128)} %refs_0_.3, s32[2]{0:T(128)} %pad_add_fusion.place_ref.refs_1_, f32[2048,128]{1,0:T(8,128)} %bitcast.9, f32[2048,128]{1,0:T(8,128)} %bitcast.12, f32[8,128]{1,0:T(8,128)} %get-tuple-element.23.refs_4_, f32[8,80,1024]{2,1,0:T(8,128)} %get-tuple-element.24.refs_5_, ...), custom_call_target="tpu_custom_call" | custom-call | tf_op jit(solution)/shard_map/serial_kernel/pallas_call | solution.py:646
Async XLA Ops:
  2.1 20.4 %all-to-all-start = ((f32[64,36,2]{1,2,0:T(2,128)}), f32[64,36,2]{1,2,0:T(2,128)S(1)}, u32[]{:S(2)}, u32[]{:S(2)}) async-start(f32[64,36,2]{1,2,0:T(2,128)} %broadcast_in_dim.6), calls=%async_computation | async-start | bytes 131072 | tf_op jit(solution)/shard_map/all_to_all | solution.py:32
  27.6 3.2 %collective-permute-start = (f32[32,128]{1,0:T(8,128)}, f32[32,128]{1,0:T(8,128)S(1)}, u32[]{:S(2)}, u32[]{:S(2)}) collective-permute-start(f32[32,128]{1,0:T(8,128)} %get-tuple-element.20), channel_id=1, source_target_pairs={{0,1},{1,0},{2,3},{3,2},{4,5},{5,4},{6,7},{7,6},{8,9},{9,8},{10,11... | collective-permute-start | bytes 49160 | tf_op jit(solution)/shard_map/ppermute | solution.py:589
  31.5 5.8 %copy-start.2 = (f32[32,128]{1,0:T(8,128)}, f32[32,128]{1,0:T(8,128)S(1)}, u32[]{:S(2)}) copy-start(f32[32,128]{1,0:T(8,128)S(1)} %add.11.refs_2_) | copy-start | bytes 49156
  32.6 22.4 %all-to-all-start.1 = ((f32[64,32,128]{2,1,0:T(8,128)}), f32[64,32,128]{2,1,0:T(8,128)S(1)}, u32[]{:S(2)}, u32[]{:S(2)}) async-start(f32[64,32,128]{2,1,0:T(8,128)} %broadcast_in_dim.7), calls=%async_computation.1 | async-start | bytes 2097152 | tf_op jit(solution)/shard_map/all_to_all | solution.py:32
  55.0 4.2 %copy-start = (f32[64,32,128]{2,1,0:T(8,128)}, f32[64,32,128]{2,1,0:T(8,128)S(1)}, u32[]{:S(2)}) copy-start(f32[64,32,128]{2,1,0:T(8,128)S(1)} %all-to-all-done.1) | copy-start | bytes 3145732
  55.0 4.2 %collective-permute-start.1 = (f32[64,32,128]{2,1,0:T(8,128)S(1)}, f32[64,32,128]{2,1,0:T(8,128)S(1)}, u32[]{:S(2)}, u32[]{:S(2)}) collective-permute-start(f32[64,32,128]{2,1,0:T(8,128)S(1)} %all-to-all-done.1), channel_id=1, source_target_pairs={{0,1},{1,0},{2,3},{3,2},{4,5},{5,4},{6,7},{7,6},{8,9},{9,8},{10,11... | collective-permute-start | bytes 3145736 | tf_op jit(solution)/shard_map/ppermute | solution.py:639
  59.3 1.0 copy-start.1
